TPU v7x, 128 devices: a whole 4x4x4 slice. The times are simulated.
128 devices in a mesh: expert: 64 (over x, y_lo, z, core), hidden: 2 (over y_hi).
Axes of the slice: x: 4, y: 4 (y_hi: 2, y_lo: 2; y = y_hi * 2 + y_lo), z: 4, core: 2. Of those that a mesh axis runs over, the one named last changes fastest.
Arguments:
- tokens: bfloat16 [256, 256, 1024], P(('expert', 'hidden')), may hold values from -24 to 24
- router: bfloat16 [1024, 256], replicated, may hold values from -2 to 2
- out_grad: bfloat16 [256, 256, 1024], P(('expert', 'hidden')), may hold values from -24 to 24
- slot_outputs: bfloat16 [256, 256, 1024], P(('expert', 'hidden')), may hold values from -6 to 6
- preact: bfloat16 [128, 512, 4096], P('expert', None, 'hidden'), may hold values from -6 to 6
- w_in: bfloat16 [128, 1024, 4096], P('expert', None, 'hidden'), may hold values from -0.1875 to 0.1875
- w_out: bfloat16 [128, 4096, 1024], P('expert', 'hidden'), may hold values from -0.09375 to 0.09375
Outputs:
- grad_tokens: bfloat16 [256, 256, 1024], P(('expert', 'hidden'))
- grad_router: float32 [1024, 256], P(('expert', 'hidden'))
All inputs are finite; a program needn't handle non-finite values.
Results may differ from a plain program's by a relative error of at most 0.017.
Values may be sent and summed in bfloat16 or wider, within the bound.
No kernel may reach another device: no remote copies, remote signals or barrier semaphores. Data moves between devices by JAX's collectives and lax.ppermute only.
A program may use at most 128 MiB of HBM per device.

v0:
```python
import jax
import jax.numpy as jnp
from jax import lax
from jax.sharding import PartitionSpec as P

gelu_coef = 0.7978845608028654
cubic_coef = 0.044715


def gelu_slope(values):
    inner = gelu_coef * (values + cubic_coef * values * values * values)
    tanh_part = jnp.tanh(inner)
    return 0.5 * (1.0 + tanh_part) + 0.5 * values * (1.0 - tanh_part * tanh_part) * gelu_coef * (
        1.0 + 3.0 * cubic_coef * values * values
    )


def shards(tokens, router, out_grad, slot_outputs, preact, w_in, w_out):
    n_exp = lax.axis_size("expert")
    n_hid = lax.axis_size("hidden")
    own_images = tokens.shape[0]
    feat_dim = tokens.shape[2]
    slot_count = router.shape[1]
    exp_dev = w_in.shape[0]
    experts_all = exp_dev * n_exp
    per_expert = slot_count // experts_all
    all_images = own_images * n_exp * n_hid
    logits = jnp.einsum("bmd,dn->bmn", tokens, router, preferred_element_type=jnp.float32)
    dispatch = jax.nn.softmax(logits, axis=1)
    combine = jax.nn.softmax(logits, axis=2)
    dispatch_b = dispatch.astype(jnp.bfloat16)
    combine_b = combine.astype(jnp.bfloat16)
    grad_combine = jnp.einsum(
        "bmd,bnd->bmn", out_grad, slot_outputs, preferred_element_type=jnp.float32
    )
    slot_grad = jnp.einsum(
        "bmn,bmd->bnd", combine_b, out_grad, preferred_element_type=jnp.float32
    ).astype(jnp.bfloat16)
    outbound = slot_grad.reshape(1, 1, own_images, experts_all, per_expert, feat_dim)
    arrived = lax.all_to_all(outbound, "expert", split_axis=3, concat_axis=0, tiled=True)
    paired = lax.all_gather(arrived, "hidden", axis=1, tiled=True)
    grads = paired.reshape(all_images, exp_dev, per_expert, feat_dim)
    saved_pre = preact.reshape(exp_dev, all_images, per_expert, preact.shape[2])
    grad_act = jnp.einsum("besd,ehd->ebsh", grads, w_out, preferred_element_type=jnp.float32)
    grad_pre = (grad_act * gelu_slope(saved_pre.astype(jnp.float32))).astype(jnp.bfloat16)
    partial_in = jnp.einsum("ebsh,edh->besd", grad_pre, w_in, preferred_element_type=jnp.float32)
    partial_in = partial_in.reshape(n_exp, n_hid, own_images, exp_dev, per_expert, feat_dim)
    summed = lax.psum_scatter(
        partial_in.astype(jnp.bfloat16), "hidden", scatter_dimension=1, tiled=True
    )
    returned = lax.all_to_all(summed, "expert", split_axis=0, concat_axis=3, tiled=True)
    slot_in_grad = returned.reshape(own_images, slot_count, feat_dim)
    grad_dispatch = jnp.einsum(
        "bmd,bnd->bmn", tokens, slot_in_grad, preferred_element_type=jnp.float32
    )
    part_disp = dispatch * (
        grad_dispatch - jnp.sum(dispatch * grad_dispatch, axis=1, keepdims=True)
    )
    part_comb = combine * (grad_combine - jnp.sum(combine * grad_combine, axis=2, keepdims=True))
    grad_logits = (part_disp + part_comb).astype(jnp.bfloat16)
    through_slots = jnp.einsum(
        "bmn,bnd->bmd", dispatch_b, slot_in_grad, preferred_element_type=jnp.float32
    )
    through_router = jnp.einsum(
        "bmn,dn->bmd", grad_logits, router, preferred_element_type=jnp.float32
    )
    grad_tokens = (through_slots + through_router).astype(jnp.bfloat16)
    router_term = jnp.einsum(
        "bmd,bmn->dn", tokens, grad_logits, preferred_element_type=jnp.float32
    ) * (1.0 / all_images)
    grad_router = lax.psum_scatter(
        router_term, ("expert", "hidden"), scatter_dimension=0, tiled=True
    )
    return (grad_tokens, grad_router)


def solution(mesh):
    in_specs = (
        P(("expert", "hidden"), None, None),
        P(),
        P(("expert", "hidden"), None, None),
        P(("expert", "hidden"), None, None),
        P("expert", None, "hidden"),
        P("expert", None, "hidden"),
        P("expert", "hidden", None),
    )
    out_specs = (P(("expert", "hidden"), None, None), P(("expert", "hidden"), None))
    return jax.shard_map(shards, mesh=mesh, in_specs=in_specs, out_specs=out_specs, check_vma=False)
```

profile of v0, /device:TPU:1, one launch (start us, length us, event | category | flops | bytes accessed | tf_op | source)
XLA Modules:
  0.0 829.3 jit_solution(8039420208504648470)
XLA Ops:
  7.2 0.0 all-gather.3.cloned.1.call-start
  7.2 1.9 fusion.41
  9.1 1.0 fusion.53
  10.1 2.2 convolution_convert_fusion
  12.3 1.5 reshape.25
  13.8 0.7 copy.60
  14.5 28.6 %all_to_all.33 = bf16[1,1,2,128,2,1024]{5,4,2,1,0,3:T(2,128)(2,1)S(1)} all-to-all(bf16[1,1,2,128,2,1024]{5,4,2,1,0,3:T(2,128)(2,1)S(1)} %copy.60), channel_id=1, replica_groups=mesh['expert'=64,'hidden'=2] {'expert'}, dimensions={3} | all-to-all | bytes 2097152 | tf_op jit(solution)/shard_map/all_to_all | solution.py:40
  43.1 0.7 copy.61
  43.8 1.3 copy.62
  45.1 0.0 reduce-scatter.5.cloned.1.call-start
  45.2 10.2 %copy.65 = f32[2,512,2048]{2,0,1:T(2,128)} copy(bf16[2,512,2048]{2,1,0:T(8,128)(2,1)} %param.11) | data formatting | bytes 12582912 | tf_op jit(solution)/shard_map/convert_element_type | solution.py:45
  55.4 24.9 %all-gather.3.cloned.1.call-done = bf16[64,2,1,2,2,2,1024]{6,0,5,4,3,2,1:T(8,128)(2,1)} async-done(((bf16[64,1,1,2,2,2,1024]{6,0,5,4,3,2,1:T(8,128)(2,1)}), bf16[64,2,1,2,2,2,1024]{6,0,5,4,3,2,1:T(8,128)(2,1)}) %all-gather.3.cloned.1.call-update) | async-done | bytes 2097168 | tf_op jit(solution)/shard_map/all_gather | solution.py:41
  80.2 3.8 copy.63
  84.0 10.7 %fusion.13 = f32[2,256,2,2048]{3,1,2,0:T(8,128)} fusion(bf16[2,2048,1024]{2,1,0:T(8,128)(2,1)} %param.13, bf16[256,2,2,1024]{3,2,1,0:T(2,128)(2,1)S(1)} %bitcast.58), kind=kOutput, calls=%fused_computation.15 | convolution fusion | flops 4294967296 | bytes 18874368 | tf_op jit(solution)/shard_map/besd,ehd->ebsh/dot_general | solution.py:44
  94.7 18.2 %convert_bitcast_fusion = bf16[256,2,2,1024]{3,0,2,1:T(8,128)(2,1)} fusion(bf16[2,1024,2048]{2,1,0:T(8,128)(2,1)} %param.12, f32[2,256,2,2048]{3,1,2,0:T(8,128)} %fusion.13, f32[2,256,2,2048]{3,0,2,1:T(2,128)} %bitcast.56), kind=kOutput, calls=%fused_computation.19 | convolution fusion | flops 4335861760 | bytes 27262976 | tf_op jit(solution)/shard_map/ebsh,edh->besd/dot_general | solution.py:46
  112.8 2.7 convert_element_type.41
  115.6 2.0 copy.73
  117.6 0.0 reduce-scatter.5.cloned.1.call-update
  117.6 35.4 %reduce-scatter.5.cloned.1.call-done = bf16[64,1,2,2,2,1024]{5,0,4,3,2,1:T(8,128)(2,1)} async-done(((bf16[64,2,2,2,2,1024]{5,0,4,3,2,1:T(8,128)(2,1)}), bf16[64,1,2,2,2,1024]{5,0,4,3,2,1:T(8,128)(2,1)}) %reduce-scatter.5.cloned.1.call-update) | async-done | bytes 1048592 | tf_op jit(solution)/shard_map/reduce_scatter | solution.py:48
  153.0 3.3 copy.74
  156.3 8.1 all-to-all-start.1
  164.4 0.3 reduce-scatter.7.cloned.1.call-start
  164.7 2.1 fusion.54
  166.8 3.8 fusion.31
  170.6 11.8 %all-to-all-done.1 = bf16[64,1,2,2,2,1024]{5,2,1,4,3,0:T(2,128)(2,1)S(1)} async-done(((bf16[64,1,2,2,2,1024]{5,2,1,4,3,0:T(2,128)(2,1)}), bf16[64,1,2,2,2,1024]{5,2,1,4,3,0:T(2,128)(2,1)S(1)}, u32[]{:S(2)}, u32[]{:S(2)}) %all-to-all-start.1) | async-done | bytes 1048608 | tf_op jit(solution)/shard_map/all_to_all | solution.py:51
  182.4 1.3 convolution_bitcast_fusion.1
  183.6 3.3 fusion.22
  186.9 2.5 copy.86
  189.5 0.0 reduce-scatter.7.cloned.1.call-update
  189.5 2.2 fusion.38
  191.7 3.3 add_convert_fusion
  195.0 627.7 %reduce-scatter.7.cloned.1.call-done = f32[8,256]{1,0:T(8,128)} async-done(((f32[1024,256]{1,0:T(8,128)}), f32[8,256]{1,0:T(8,128)}) %reduce-scatter.7.cloned.1.call-update) | async-done | bytes 8208
  (9 shorter events, 0.0 us)
Async XLA Ops:
  7.2 2.9 copy-start
  7.2 73.0 %all-gather.3.cloned.1.call-start = ((), (), s32[]{:S(2)}) async-start(), calls=%async_computation.5 | async-start | bytes 3145728 | tf_op jit(solution)/shard_map/all_gather | solution.py:41
  9.1 46.2 %copy-start.1 = (f32[2,256,256]{2,1,0:T(8,128)}, f32[2,256,256]{2,1,0:T(8,128)S(1)}, u32[]{:S(2)}) copy-start(f32[2,256,256]{2,1,0:T(8,128)S(1)} %fusion.41) | copy-start | bytes 1572868
  45.1 107.9 %reduce-scatter.5.cloned.1.call-start = ((), (), s32[]{:S(2)}) async-start(), calls=%async_computation.4 | async-start | bytes 3145728 | tf_op jit(solution)/shard_map/reduce_scatter | solution.py:48
  117.5 64.8 %copy-start.2 = (bf16[2,256,1024]{2,1,0:T(8,128)(2,1)S(1)}, bf16[2,256,1024]{2,1,0:T(8,128)(2,1)}, u32[]{:S(2)}) copy-start(bf16[2,256,1024]{2,1,0:T(8,128)(2,1)} %param.7) | copy-start | bytes 3145732
  156.3 26.0 %all-to-all-start.1 = ((bf16[64,1,2,2,2,1024]{5,2,1,4,3,0:T(2,128)(2,1)}), bf16[64,1,2,2,2,1024]{5,2,1,4,3,0:T(2,128)(2,1)S(1)}, u32[]{:S(2)}, u32[]{:S(2)}) async-start(bf16[64,1,2,2,2,1024]{5,2,1,4,3,0:T(2,128)(2,1)} %copy.74), calls=%async_computation.2 | async-start | bytes 2097152 | tf_op jit(solution)/shard_map/all_to_all | solution.py:51
  164.4 658.3 %reduce-scatter.7.cloned.1.call-start = ((), (), s32[]{:S(2)}) async-start(), calls=%async_computation.6 | async-start | bytes 1056768
  182.4 7.1 copy-start.3
Sparse Core Ops, SparseCore 0:
  45.3 34.9 all-gather.2
  117.7 35.2 reduce-scatter.4
  189.6 633.0 reduce-scatter.6
where the time goes:
time: 832 us; the launch traced here: 829 us
  waiting for transfers between devices  700 us (84%)
  matrix products  46.8 us (6%)
  local copies, waits for them, and re-layouts  28.7 us (3%)
  blocking collectives  28.6 us (3%)
  between operations  13.8 us (2%)
  starting transfers between devices  8.44 us (1%)
    unnamed x4, waiting for transfers between devices  628 us
    reduce_scatter x1, waiting for transfers between devices, shards(): lax.psum_scatter(partial_in.astype(jnp.bfloat16), 'hidden', scatter_dimen...  35.4 us
    all_to_all x1, blocking collectives, shards(): lax.all_to_all(outbound, 'expert', split_axis=3, concat_axis=0, tiled=True)  28.6 us
    all_gather x1, waiting for transfers between devices, shards(): paired = lax.all_gather(arrived, 'hidden', axis=1, tiled=True)  24.9 us
    dot_general x1, matrix products, shards(): jnp.einsum('ebsh,edh->besd', grad_pre, w_in, preferred_element_type=jnp.f...  18.2 us
  transfers between devices with their start and end apart: 4, of which 4 were waited for; matrix products, arithmetic and copies ran while one was open for 3% of the time, Pallas kernels for 0%

commit v1 on v0

--- a/solution.py
+++ b/solution.py
@@ -36,20 +36,26 @@
     slot_grad = jnp.einsum(
         "bmn,bmd->bnd", combine_b, out_grad, preferred_element_type=jnp.float32
     ).astype(jnp.bfloat16)
-    outbound = slot_grad.reshape(1, 1, own_images, experts_all, per_expert, feat_dim)
-    arrived = lax.all_to_all(outbound, "expert", split_axis=3, concat_axis=0, tiled=True)
-    paired = lax.all_gather(arrived, "hidden", axis=1, tiled=True)
-    grads = paired.reshape(all_images, exp_dev, per_expert, feat_dim)
-    saved_pre = preact.reshape(exp_dev, all_images, per_expert, preact.shape[2])
-    grad_act = jnp.einsum("besd,ehd->ebsh", grads, w_out, preferred_element_type=jnp.float32)
-    grad_pre = (grad_act * gelu_slope(saved_pre.astype(jnp.float32))).astype(jnp.bfloat16)
-    partial_in = jnp.einsum("ebsh,edh->besd", grad_pre, w_in, preferred_element_type=jnp.float32)
-    partial_in = partial_in.reshape(n_exp, n_hid, own_images, exp_dev, per_expert, feat_dim)
-    summed = lax.psum_scatter(
-        partial_in.astype(jnp.bfloat16), "hidden", scatter_dimension=1, tiled=True
-    )
-    returned = lax.all_to_all(summed, "expert", split_axis=0, concat_axis=3, tiled=True)
-    slot_in_grad = returned.reshape(own_images, slot_count, feat_dim)
+    devs = n_exp * n_hid
+    rows = exp_dev * own_images * per_expert
+    both = ("expert", "hidden")
+    outbound = slot_grad.reshape(own_images, n_exp, exp_dev, per_expert, feat_dim)
+    outbound = outbound.transpose(1, 2, 0, 3, 4).reshape(n_exp, 1, rows, feat_dim)
+    outbound = jnp.broadcast_to(outbound, (n_exp, n_hid, rows, feat_dim))
+    outbound = outbound.reshape(devs, rows, feat_dim)
+    arrived = lax.all_to_all(outbound, both, split_axis=0, concat_axis=0, tiled=True)
+    arrived = arrived.reshape(devs, exp_dev, own_images * per_expert, feat_dim)
+    grads = arrived.transpose(1, 0, 2, 3).reshape(exp_dev, -1, feat_dim)
+    grad_act = jnp.einsum("erd,ehd->erh", grads, w_out, preferred_element_type=jnp.float32)
+    grad_pre = (grad_act * gelu_slope(preact.astype(jnp.float32))).astype(jnp.bfloat16)
+    partial_in = jnp.einsum("erh,edh->erd", grad_pre, w_in, preferred_element_type=jnp.float32)
+    partial_in = partial_in.astype(jnp.bfloat16).reshape(exp_dev, devs, -1, feat_dim)
+    partial_in = partial_in.transpose(1, 0, 2, 3).reshape(devs, rows, feat_dim)
+    returned = lax.all_to_all(partial_in, both, split_axis=0, concat_axis=0, tiled=True)
+    returned = returned.reshape(n_exp, n_hid, rows, feat_dim).astype(jnp.float32)
+    summed = jnp.sum(returned, axis=1).astype(jnp.bfloat16)
+    summed = summed.reshape(n_exp, exp_dev, own_images, per_expert, feat_dim)
+    slot_in_grad = summed.transpose(2, 0, 1, 3, 4).reshape(own_images, slot_count, feat_dim)
     grad_dispatch = jnp.einsum(
         "bmd,bnd->bmn", tokens, slot_in_grad, preferred_element_type=jnp.float32
     )
@@ -68,9 +74,9 @@
     router_term = jnp.einsum(
         "bmd,bmn->dn", tokens, grad_logits, preferred_element_type=jnp.float32
     ) * (1.0 / all_images)
-    grad_router = lax.psum_scatter(
-        router_term, ("expert", "hidden"), scatter_dimension=0, tiled=True
-    )
+    pieces = router_term.astype(jnp.bfloat16).reshape(devs, feat_dim // devs, slot_count)
+    pieces = lax.all_to_all(pieces, both, split_axis=0, concat_axis=0, tiled=True)
+    grad_router = jnp.sum(pieces.astype(jnp.float32), axis=0)
     return (grad_tokens, grad_router)
 
 

time: 832 us -> 138 us (0.17)
  waiting for transfers between devices: 700 us -> 30.5 us
  local copies, waits for them, and re-layouts: 28.7 us -> 14.5 us
  between operations: 13.8 us -> 0.77 us
  blocking collectives: 28.6 us -> 41 us
  matrix products: 46.8 us -> 36.1 us
    unnamed x4 -> x0, waiting for transfers between devices: 628 us -> none
    reduce_scatter x1 -> x0, waiting for transfers between devices: 35.4 us -> none  [shards(): lax.psum_scatter(partial_in.astype(jnp.bfloat16), 'hidden', scatter_dimen...]
    all_gather x1 -> x0, waiting for transfers between devices: 24.9 us -> none  [shards(): paired = lax.all_gather(arrived, 'hidden', axis=1, tiled=True)]
    all_to_all x1 -> x2, waiting for transfers between devices: 11.8 us -> 30.5 us  [the longest x1 23.9 us: shards(): lax.all_to_all(partial_in, both, split_axis=0, concat_axis=0, tiled=True)]
    convert_element_type x3 -> x1, local copies, waits for them, and re-layouts: 14.9 us -> 1.02 us  [shards(): router_term.astype(jnp.bfloat16).reshape(devs, feat_dim // devs, slot_count)]
    dot_general x2 -> x1, matrix products: 28.8 us -> 16.1 us  [shards(): jnp.einsum('erh,edh->erd', grad_pre, w_in, preferred_element_type=jnp.flo...]
    all_to_all x1, blocking collectives: 28.6 us -> 41 us  [shards(): lax.all_to_all(outbound, both, split_axis=0, concat_axis=0, tiled=True)]
  transfers between devices with their start and end apart: 4 -> 2, of which waited for: 4 -> 2; matrix products, arithmetic and copies ran while one was open for 3% -> 9% of each run, Pallas kernels for 0% -> 0%
where the time goes in v1:
time: 138 us; the launch traced here: 137 us
  blocking collectives  41 us (30%)
  matrix products  36.1 us (26%)
  waiting for transfers between devices  30.5 us (22%)
  local copies, waits for them, and re-layouts  14.5 us (11%)
  starting transfers between devices  10.3 us (7%)
  other arithmetic  4.32 us (3%)
    all_to_all x1, blocking collectives, shards(): lax.all_to_all(outbound, both, split_axis=0, concat_axis=0, tiled=True)  41 us
    all_to_all x1, waiting for transfers between devices, shards(): lax.all_to_all(partial_in, both, split_axis=0, concat_axis=0, tiled=True)  23.9 us
    dot_general x1, matrix products, shards(): jnp.einsum('erh,edh->erd', grad_pre, w_in, preferred_element_type=jnp.flo...  16.1 us
    all_to_all x1, waiting for transfers between devices, shards(): lax.all_to_all(pieces, both, split_axis=0, concat_axis=0, tiled=True)  6.65 us
    all_to_all x1, starting transfers between devices, shards(): lax.all_to_all(partial_in, both, split_axis=0, concat_axis=0, tiled=True)  5.13 us
    all_to_all x1, starting transfers between devices, shards(): lax.all_to_all(pieces, both, split_axis=0, concat_axis=0, tiled=True)  5.13 us
    dot_general x1, matrix products, shards(): jnp.einsum('bmn,dn->bmd', grad_logits, router, preferred_element_type=jnp...  3.91 us
    sub x1, matrix products, shards(): grad_combine - jnp.sum(combine * grad_combine, axis=2, keepdims=True)  3.65 us
  transfers between devices with their start and end apart: 2, of which 2 were waited for; matrix products, arithmetic and copies ran while one was open for 9% of the time, Pallas kernels for 0%

profile of v1, /device:TPU:1, one launch (start us, length us, event | category | flops | bytes accessed | tf_op | source)
XLA Modules:
  0.0 137.5 jit_solution(2255640039018739524)
XLA Ops:
  0.6 0.0 copy-start
  0.6 1.9 %fusion.40 = f32[2,256,256]{2,1,0:T(8,128)S(1)} fusion(bf16[2,256,1024]{2,1,0:T(8,128)(2,1)} %param.7, bf16[1024,256]{1,0:T(8,128)(2,1)} %param.8), kind=kOutput, calls=%fused_computation.49 | convolution fusion | flops 268435456 | bytes 2097152 | tf_op jit(solution)/shard_map/bmd,dn->bmn/dot_general | solution.py:28
  2.5 1.0 fusion.52
  3.5 2.2 %convolution_convert_fusion = bf16[2,256,1024]{2,1,0:T(8,128)(2,1)} fusion(bf16[2,256,1024]{2,1,0:T(8,128)(2,1)S(1)} %copy-done, f32[2,256]{1,0:T(2,128)S(1)} %get-tuple-element.2, f32[2,256,256]{2,1,0:T(8,128)S(1)} %fusion.40), kind=kOutput, calls=%fused_computation.25 | convolution fusion | flops 269353728 | bytes 2623488 | tf_op jit(solution)/shard_map/bmn,bmd->bnd/dot_general | solution.py:36
  5.7 1.5 %reshape.42 = bf16[2,64,2,2,1024]{4,3,2,1,0:T(2,128)(2,1)S(1)} reshape(bf16[2,256,1024]{2,1,0:T(8,128)(2,1)} %convolution_convert_fusion) | data formatting | bytes 2097152 | tf_op jit(solution)/shard_map/reshape | solution.py:42
  7.2 0.3 copy.49
  7.5 0.6 copy.50
  8.1 0.3 broadcast_in_dim.5
  8.4 41.0 %all_to_all.15 = bf16[128,8,1024]{2,1,0:T(8,128)(2,1)S(1)} all-to-all(bf16[128,8,1024]{2,1,0:T(8,128)(2,1)S(1)} %bitcast.49), channel_id=1, replica_groups=mesh['expert'=64,'hidden'=2] {'expert','hidden'}, dimensions={0} | all-to-all | bytes 4194304 | tf_op jit(solution)/shard_map/all_to_all | solution.py:46
  49.4 0.0 copy-done.1
  49.4 1.2 copy.51
  50.5 2.2 %copy.52 = bf16[2,128,4,1024]{3,0,2,1:T(2,128)(2,1)S(1)} copy(bf16[2,128,4,1024]{3,1,2,0:T(8,128)(2,1)S(1)} %bitcast.50) | data formatting | bytes 4194304 | tf_op jit(solution)/shard_map/transpose | solution.py:48
  52.7 16.1 %fusion.16 = bf16[2,512,1024]{2,1,0:T(8,128)(2,1)} fusion(bf16[2,1024,2048]{2,1,0:T(8,128)(2,1)} %param.12, bf16[2,512,2048]{2,1,0:T(8,128)(2,1)} %param.11, bf16[2,2048,1024]{2,1,0:T(8,128)(2,1)} %param.13, bf16[2,512,1024]{2,0,1:T(2,128)(2,1)S(1)} %bitcast.54), kind=kOutput, calls=%fused_computation.24 | convolution fusion | flops 8632926208 | bytes 25165824 | tf_op jit(solution)/shard_map/erh,edh->erd/dot_general | solution.py:51
  68.8 2.7 %reshape.46 = bf16[2,128,4,1024]{3,2,1,0:T(4,128)(2,1)S(1)} reshape(bf16[2,512,1024]{2,1,0:T(8,128)(2,1)} %fusion.16) | data formatting | bytes 4194304 | tf_op jit(solution)/shard_map/reshape | solution.py:52
  71.6 0.6 copy.54
  72.2 2.5 %copy.55 = bf16[128,8,1024]{2,1,0:T(8,128)(2,1)} copy(bf16[128,8,1024]{2,0,1:T(8,128)(2,1)S(1)} %bitcast.51) | data formatting | bytes 4194304 | tf_op jit(solution)/shard_map/reshape | solution.py:53
  74.7 5.1 %all-to-all-start.1 = ((bf16[128,8,1024]{2,1,0:T(8,128)(2,1)}), bf16[128,8,1024]{2,1,0:T(8,128)(2,1)S(1)}, u32[]{:S(2)}, u32[]{:S(2)}) async-start(bf16[128,8,1024]{2,1,0:T(8,128)(2,1)} %copy.55), calls=%async_computation.1 | async-start | bytes 4194304 | tf_op jit(solution)/shard_map/all_to_all | solution.py:54
  79.9 2.1 %fusion.53 = (f32[2,256]{1,0:T(2,128)S(1)}, f32[2,256,256]{2,1,0:T(8,128)}) fusion(f32[2,256,256]{2,1,0:T(8,128)} %copy-done.1), kind=kOutput, calls=%fused_computation.65 | output fusion | flops 262399 | bytes 1050624 | tf_op jit(solution)/shard_map/sub | solution.py:29
  82.0 3.7 %fusion.30 = f32[2,256,256]{2,1,0:T(8,128)} fusion(f32[2,256,256]{2,1,0:T(8,128)} %get-tuple-element.3, f32[2,256]{1,0:T(2,128)S(1)} %get-tuple-element.2, bf16[2,256,1024]{2,1,0:T(8,128)(2,1)S(1)} %copy-done, bf16[2,256,1024]{2,1,0:T(8,128)(2,1)} %param.10), kind=kOutput, calls=%fused_computation.39 | convolution fusion | flops 537527040 | bytes 3147776 | tf_op jit(solution)/shard_map/sub | solution.py:65
  85.7 23.9 %all-to-all-done.1 = bf16[128,8,1024]{2,1,0:T(8,128)(2,1)S(1)} async-done(((bf16[128,8,1024]{2,1,0:T(8,128)(2,1)}), bf16[128,8,1024]{2,1,0:T(8,128)(2,1)S(1)}, u32[]{:S(2)}, u32[]{:S(2)}) %all-to-all-start.1) | async-done | bytes 2097184 | tf_op jit(solution)/shard_map/all_to_all | solution.py:54
  109.6 0.5 bitcast_reduce_fusion
  110.0 0.0 copy-start.2
  110.0 0.6 copy.56
  110.6 1.1 copy.57
  111.7 2.5 %convolution_bitcast_fusion.1 = f32[2,256,256]{2,1,0:T(8,128)} fusion(bf16[2,256,1024]{2,1,0:T(8,128)(2,1)} %param.7, bf16[2,256,1024]{2,0,1:T(2,128)(2,1)S(1)} %bitcast.55), kind=kOutput, calls=%fused_computation.31 | convolution fusion | flops 268435456 | bytes 2621440 | tf_op jit(solution)/shard_map/bmd,bnd->bmn/dot_general | solution.py:59
  114.2 2.6 %fusion.25 = bf16[1024,256]{0,1:T(8,128)(2,1)S(1)} fusion(bf16[2,256,1024]{2,1,0:T(8,128)(2,1)} %param.7, f32[2,256,256]{2,1,0:T(8,128)} %fusion.30, f32[2,256,256]{2,1,0:T(8,128)} %convolution_bitcast_fusion.1, f32[2,256,256]{2,1,0:T(8,128)} %get-tuple-element.5, f32[2,256]{1,0:T(2,128)S(1)} %get-tuple-element.4), kind=kOutput, calls=%fused_computation.34 | convolution fusion | flops 269878016 | bytes 3147776 | tf_op jit(solution)/shard_map/bmd,bmn->dn/dot_general | solution.py:74
  116.8 1.0 copy.63
  117.9 5.1 %all-to-all-start.2 = ((bf16[128,8,256]{2,1,0:T(8,128)(2,1)}), bf16[128,8,256]{2,1,0:T(8,128)(2,1)S(1)}, u32[]{:S(2)}, u32[]{:S(2)}) async-start(bf16[128,8,256]{2,1,0:T(8,128)(2,1)} %bitcast.16), calls=%async_computation.2 | async-start | bytes 1048576 | tf_op jit(solution)/shard_map/all_to_all | solution.py:78
  123.0 3.2 %fusion.37 = f32[2,256,1024]{2,1,0:T(8,128)} fusion(bf16[2,256,1024]{2,0,1:T(2,128)(2,1)S(1)} %bitcast.56, f32[2,256]{1,0:T(2,128)S(1)} %get-tuple-element.4, f32[2,256,256]{2,1,0:T(8,128)} %copy-done.1), kind=kOutput, calls=%fused_computation.46 | convolution fusion | flops 268829440 | bytes 3672064 | tf_op jit(solution)/shard_map/bmn,bnd->bmd/dot_general | solution.py:67
  126.2 3.9 %add_convert_fusion = bf16[2,256,1024]{2,1,0:T(8,128)(2,1)} fusion(f32[2,256,1024]{2,1,0:T(8,128)} %fusion.37, f32[2,256,256]{2,1,0:T(8,128)} %fusion.30, f32[2,256,256]{2,1,0:T(8,128)} %convolution_bitcast_fusion.1, bf16[1024,256]{1,0:T(8,128)(2,1)S(1)} %copy-done.2, f32[2,256,256]{2,1,0:T(8,128)} %get-tuple-element.5, f32[2,256]{1,0:T(2,128)S(1)} %get-tuple-element.4), kind=kOutput, calls=%fused_computation.23 | convolution fusion | flops 270402304 | bytes 5244928 | tf_op jit(solution)/shard_map/bmn,dn->bmd/dot_general | solution.py:70
  130.1 6.7 %all-to-all-done.2 = bf16[128,8,256]{2,1,0:T(8,128)(2,1)S(1)} async-done(((bf16[128,8,256]{2,1,0:T(8,128)(2,1)}), bf16[128,8,256]{2,1,0:T(8,128)(2,1)S(1)}, u32[]{:S(2)}, u32[]{:S(2)}) %all-to-all-start.2) | async-done | bytes 524320 | tf_op jit(solution)/shard_map/all_to_all | solution.py:78
  136.8 0.7 convert_reduce_fusion
  (3 shorter events, 0.0 us)
Async XLA Ops:
  0.6 2.9 %copy-start = (bf16[2,256,1024]{2,1,0:T(8,128)(2,1)S(1)}, bf16[2,256,1024]{2,1,0:T(8,128)(2,1)}, u32[]{:S(2)}) copy-start(bf16[2,256,1024]{2,1,0:T(8,128)(2,1)} %param.9) | copy-start | bytes 3145732
  2.5 46.8 %copy-start.1 = (f32[2,256,256]{2,1,0:T(8,128)}, f32[2,256,256]{2,1,0:T(8,128)S(1)}, u32[]{:S(2)}) copy-start(f32[2,256,256]{2,1,0:T(8,128)S(1)} %fusion.40) | copy-start | bytes 1572868
  74.7 34.8 %all-to-all-start.1 = ((bf16[128,8,1024]{2,1,0:T(8,128)(2,1)}), bf16[128,8,1024]{2,1,0:T(8,128)(2,1)S(1)}, u32[]{:S(2)}, u32[]{:S(2)}) async-start(bf16[128,8,1024]{2,1,0:T(8,128)(2,1)} %copy.55), calls=%async_computation.1 | async-start | bytes 4194304 | tf_op jit(solution)/shard_map/all_to_all | solution.py:54
  110.0 16.2 %copy-start.2 = (bf16[1024,256]{1,0:T(8,128)(2,1)S(1)}, bf16[1024,256]{1,0:T(8,128)(2,1)}, u32[]{:S(2)}) copy-start(bf16[1024,256]{1,0:T(8,128)(2,1)} %param.8) | copy-start | bytes 1572868
  117.9 18.9 %all-to-all-start.2 = ((bf16[128,8,256]{2,1,0:T(8,128)(2,1)}), bf16[128,8,256]{2,1,0:T(8,128)(2,1)S(1)}, u32[]{:S(2)}, u32[]{:S(2)}) async-start(bf16[128,8,256]{2,1,0:T(8,128)(2,1)} %bitcast.16), calls=%async_computation.2 | async-start | bytes 1048576 | tf_op jit(solution)/shard_map/all_to_all | solution.py:78

commit v2 on v0

v2 whole, which is shorter than its diff:
```python
import functools

import jax
import jax.numpy as jnp
from jax import lax
from jax.experimental import pallas as pl
from jax.experimental.pallas import tpu as pltpu
from jax.sharding import PartitionSpec as P

gelu_coef = 0.7978845608028654
cubic_coef = 0.044715
bf16 = jnp.bfloat16
f32 = jnp.float32
block = 256
vmem_bytes = 40 * 1024 * 1024
in_hbm = pl.BlockSpec(memory_space=pl.ANY)
in_vmem = pl.BlockSpec(memory_space=pltpu.VMEM)


def gelu_slope(values):
    inner = gelu_coef * (values + cubic_coef * values * values * values)
    tanh_part = jnp.tanh(inner)
    return 0.5 * (1.0 + tanh_part) + 0.5 * values * (1.0 - tanh_part * tanh_part) * gelu_coef * (
        1.0 + 3.0 * cubic_coef * values * values
    )


def mm(a, b, over_a=1, over_b=0):
    return lax.dot_general(a, b, (((over_a,), (over_b,)), ((), ())), preferred_element_type=f32)


def softmax(values, axis):
    grown = jnp.exp(values - jnp.max(values, axis=axis, keepdims=True))
    return grown / jnp.sum(grown, axis=axis, keepdims=True)


def one_hot(rows, cols, source):
    r = lax.broadcasted_iota(jnp.int32, (rows, cols), 0)
    c = lax.broadcasted_iota(jnp.int32, (rows, cols), 1)
    return jnp.where(source(r) == c, 1.0, 0.0).astype(bf16)


def slots_kernel(
    tokens_hbm, router_hbm, out_grad_hbm, logits_hbm, send_hbm, tokens, router, out_grad, logits_kept, slot_grad, send,
    sems, send_sems, *, images, rows, n_hid, exp_dev, per
):
    loads = [pltpu.make_async_copy(router_hbm, router, sems.at[2 * images])]
    loads += [pltpu.make_async_copy(tokens_hbm.at[i], tokens.at[i], sems.at[i]) for i in range(images)]
    loads += [pltpu.make_async_copy(out_grad_hbm.at[i], out_grad.at[i], sems.at[images + i]) for i in range(images)]
    for load in loads:
        load.start()
    for load in loads[: images + 1]:
        load.wait()
    combine = []
    for i in range(images):
        logits = mm(tokens[i], router[...])
        logits_kept[i] = logits
        combine.append(softmax(logits, 1).astype(bf16))
    for load in loads[images + 1 :]:
        load.wait()
    for i in range(images):
        slot_grad[i] = mm(combine[i], out_grad[i], 0, 0).astype(bf16)
    own = exp_dev * per
    take = block // (n_hid * rows) * own

    def source(r):
        dest, at = r // (n_hid * rows), r % rows
        exp, img, s = at // (images * per), (at // per) % images, at % per
        return img * take + dest * own + exp * per + s

    pick = one_hot(block, images * take, source)
    copies = []
    for k in range(send.shape[0] // block):
        parts = [slot_grad[m, k * take : (k + 1) * take, :] for m in range(images)]
        at = pl.ds(k * block, block)
        send[at, :] = mm(pick, jnp.concatenate(parts, axis=0)).astype(bf16)
        copies.append(pltpu.make_async_copy(send.at[at], send_hbm.at[at], send_sems.at[k]))
        copies[-1].start()
    copies.append(pltpu.make_async_copy(logits_kept, logits_hbm, send_sems.at[len(copies)]))
    copies[-1].start()
    for copy in copies:
        copy.wait()


def experts_kernel(
    recv_ref, slope_hbm, w_in_hbm, w_out_hbm, send_hbm, slope, w_in, w_out, grads, grad_pre, back, send, sems, send_sems,
    *, exp_dev, rows
):
    hid = slope.shape[2]
    first = [pl.ds(0, hid // 4), pl.ds(hid // 4, hid // 4), pl.ds(hid // 2, hid // 2)]
    units = [first] + [[pl.ds(0, hid)]] * (exp_dev - 1)
    loads = []
    for e in range(exp_dev):
        for at in units[e]:
            loads.append((w_out_hbm.at[e, at], w_out.at[e, at]))
            loads.append((slope_hbm.at[e, :, at], slope.at[e, :, at]))
        loads.append((w_in_hbm.at[e], w_in.at[e]))
    loads = [pltpu.make_async_copy(a, b, sems.at[n]) for n, (a, b) in enumerate(loads)]
    for load in loads:
        load.start()
    own = rows // exp_dev
    take = block // exp_dev
    blocks = recv_ref.shape[0] // block
    pick = one_hot(block, block, lambda r: (r % take // own) * rows + r // take * own + r % own)
    for k in range(blocks):
        picked = mm(pick, recv_ref[k * block : (k + 1) * block, :]).astype(bf16)
        for e in range(exp_dev):
            grads[e, k * take : (k + 1) * take, :] = picked[e * take : (e + 1) * take, :]
    n = 0
    for e in range(exp_dev):
        for at in units[e]:
            loads[n].wait()
            loads[n + 1].wait()
            grad_act = mm(grads[e], w_out[e, at, :], 1, 1)
            grad_pre[:, at] = (grad_act * slope[e, :, at].astype(f32)).astype(bf16)
            n += 2
        loads[n].wait()
        back[e] = mm(grad_pre[...], w_in[e], 1, 1).astype(bf16)
        n += 1
    pick = one_hot(block, block, lambda r: (r % rows // own) * take + r // rows * own + r % own)
    copies = []
    for k in range(blocks):
        parts = [back[e, k * take : (k + 1) * take, :] for e in range(exp_dev)]
        at = pl.ds(k * block, block)
        send[at, :] = mm(pick, jnp.concatenate(parts, axis=0)).astype(bf16)
        copies.append(pltpu.make_async_copy(send.at[at], send_hbm.at[at], send_sems.at[k]))
        copies[-1].start()
    for copy in copies:
        copy.wait()


def combine_kernel(
    logits_ref, tokens_ref, out_grad_ref, slot_outputs_ref, turned_ref, dispatch_ref, weights_ref, part_ref
):
    images, toks = logits_ref.shape[:2]
    for i in range(images):
        dispatch = softmax(logits_ref[i], 0)
        dispatch_ref[i] = dispatch
        weights_ref[i] = dispatch.astype(bf16)
        combine = softmax(logits_ref[i], 1)
        grad = mm(out_grad_ref[i], slot_outputs_ref[i], 1, 1)
        part_ref[i] = combine * (grad - jnp.sum(combine * grad, axis=1, keepdims=True))
        turned_ref[:, i * toks : (i + 1) * toks] = jnp.transpose(tokens_ref[i])


def logits_kernel(
    recv_ref, tokens_hbm, turned_hbm, dispatch_hbm, part_hbm, slot_hbm, grad_hbm, router_hbm,
    tokens, turned, dispatch, part, slot_in, grad_logits, router_term, sems, *, images, rows, n_hid, exp_dev, per
):
    loads = [(tokens_hbm, tokens), (dispatch_hbm, dispatch), (part_hbm, part), (turned_hbm, turned)]
    loads = [pltpu.make_async_copy(a, b, sems.at[n]) for n, (a, b) in enumerate(loads)]
    for load in loads:
        load.start()
    feat = recv_ref.shape[1]
    own = exp_dev * per
    take = block // images

    def source(r):
        img, dest, exp, s = r // take, r % take // own, r % own // per, r % per
        return dest * rows + exp * images * per + img * per + s

    pick = one_hot(block, block, source)
    for k in range(recv_ref.shape[0] // (n_hid * block)):
        halves = recv_ref[k * n_hid * block : (k + 1) * n_hid * block, :].astype(f32)
        halves = halves.reshape(block // rows, n_hid, rows, feat)
        summed = halves[:, 0]
        for h in range(1, n_hid):
            summed = summed + halves[:, h]
        picked = mm(pick, summed.reshape(block, feat).astype(bf16)).astype(bf16)
        for i in range(images):
            slot_in[i, k * take : (k + 1) * take, :] = picked[i * take : (i + 1) * take, :]
    copies = [pltpu.make_async_copy(slot_in, slot_hbm, sems.at[len(loads)])]
    copies[-1].start()
    for load in loads[:3]:
        load.wait()
    for i in range(images):
        weights = dispatch[i]
        grad_dispatch = mm(tokens[i], slot_in[i], 1, 1)
        weighed = jnp.sum(weights * grad_dispatch, axis=0, keepdims=True)
        grad_logits[i] = (weights * (grad_dispatch - weighed) + part[i]).astype(bf16)
    copies.append(pltpu.make_async_copy(grad_logits, grad_hbm, sems.at[len(loads) + 1]))
    copies[-1].start()
    loads[3].wait()
    half = feat // 2
    for k in range(2):
        at = pl.ds(k * half, half)
        grads = jnp.concatenate([grad_logits[i] for i in range(images)], axis=0)
        router_term[at, :] = mm(turned[at, :], grads).astype(bf16)
        copies.append(pltpu.make_async_copy(router_term.at[at], router_hbm.at[at], sems.at[len(loads) + 2 + k]))
        copies[-1].start()
    for copy in copies:
        copy.wait()


def shards(tokens, router, out_grad, slot_outputs, preact, w_in, w_out):
    n_exp = lax.axis_size("expert")
    n_hid = lax.axis_size("hidden")
    both = ("expert", "hidden")
    devs = n_exp * n_hid
    images, toks, feat = tokens.shape
    slots = router.shape[1]
    exp_dev, exp_rows, hid = preact.shape
    per = slots // (exp_dev * n_exp)
    rows = images * exp_dev * per
    all_rows = devs * rows
    sizes = dict(images=images, rows=rows, n_hid=n_hid, exp_dev=exp_dev, per=per)
    dma = pltpu.SemaphoreType.DMA

    def exchange(x):
        split = x.reshape(devs, -1, x.shape[1])
        return lax.all_to_all(split, both, split_axis=0, concat_axis=0, tiled=True)

    def call(kernel, ins, outs, outs_in, scratch, flops, moved, name):
        kept = pl.pallas_call(
            kernel,
            in_specs=ins,
            out_specs=[outs_in] * len(outs),
            out_shape=[pltpu.HBM(*o) for o in outs],
            scratch_shapes=scratch,
            compiler_params=pltpu.CompilerParams(vmem_limit_bytes=vmem_bytes),
            cost_estimate=pl.CostEstimate(flops=flops, transcendentals=0, bytes_accessed=moved),
            name=name,
        )
        return lambda *xs: kept(*[hold(x) if i is in_hbm else x for i, x in zip(ins, xs)])

    def hold(x):
        return pltpu.with_memory_space_constraint(x, pltpu.HBM)

    per_image = 2 * images * toks * slots * feat
    logit_shape = (images, toks, slots)
    slot_shape = (images, slots, feat)
    logits, send = call(
        functools.partial(slots_kernel, **sizes),
        [in_hbm] * 3,
        [(logit_shape, f32), ((all_rows, feat), bf16)],
        in_hbm,
        [
            pltpu.VMEM(tokens.shape, bf16),
            pltpu.VMEM(router.shape, bf16),
            pltpu.VMEM(out_grad.shape, bf16),
            pltpu.VMEM(logit_shape, f32),
            pltpu.VMEM(slot_shape, bf16),
            pltpu.VMEM((all_rows, feat), bf16),
            dma((2 * images + 1,)),
            dma((1 + all_rows // block,)),
        ],
        2 * per_image,
        6 << 20,
        "slots",
    )(tokens, router, out_grad)

    arrived = exchange(send)
    preact, _ = lax.optimization_barrier((preact, send))
    slope = gelu_slope(preact.astype(f32)).astype(bf16)

    partial_in = call(
        functools.partial(experts_kernel, exp_dev=exp_dev, rows=rows),
        [in_vmem] + [in_hbm] * 3,
        [((all_rows, feat), bf16)],
        in_hbm,
        [
            pltpu.VMEM(preact.shape, bf16),
            pltpu.VMEM(w_in.shape, bf16),
            pltpu.VMEM(w_out.shape, bf16),
            pltpu.VMEM((exp_dev, exp_rows, feat), bf16),
            pltpu.VMEM((exp_rows, hid), bf16),
            pltpu.VMEM((exp_dev, exp_rows, feat), bf16),
            pltpu.VMEM((all_rows, feat), bf16),
            dma((3 * exp_dev + 4,)),
            dma((all_rows // block,)),
        ],
        4 * exp_dev * exp_rows * feat * hid,
        24 << 20,
        "experts",
    )(arrived.reshape(all_rows, feat), slope, w_in, w_out)[0]

    returned = exchange(partial_in)
    logits, _ = lax.optimization_barrier((logits, partial_in))
    turned, dispatch, weights, part_comb = call(
        combine_kernel,
        [in_vmem] * 4,
        [((feat, images * toks), bf16), (logit_shape, f32), (logit_shape, bf16), (logit_shape, f32)],
        in_vmem,
        [],
        per_image,
        8 << 20,
        "combine",
    )(logits, tokens, out_grad, slot_outputs)

    slot_in_grad, grad_logits, router_term = call(
        functools.partial(logits_kernel, **sizes),
        [in_vmem] + [in_hbm] * 4,
        [(slot_shape, bf16), (logit_shape, bf16), (router.shape, bf16)],
        in_hbm,
        [
            pltpu.VMEM(tokens.shape, bf16),
            pltpu.VMEM((feat, images * toks), bf16),
            pltpu.VMEM(logit_shape, f32),
            pltpu.VMEM(logit_shape, f32),
            pltpu.VMEM(slot_shape, bf16),
            pltpu.VMEM(logit_shape, bf16),
            pltpu.VMEM(router.shape, bf16),
            dma((8,)),
        ],
        3 * per_image,
        6 << 20,
        "logit_grads",
    )(returned.reshape(all_rows, feat), tokens, turned, dispatch, part_comb)

    pieces = exchange(router_term)
    through_slots = jnp.einsum("bmn,bnd->bmd", weights, slot_in_grad, preferred_element_type=f32)
    through_router = jnp.einsum("bmn,dn->bmd", grad_logits, router, preferred_element_type=f32)
    grad_tokens = (through_slots + through_router).astype(bf16)
    grad_router = jnp.sum(pieces.astype(f32) * (1.0 / (images * devs)), axis=0)
    return (grad_tokens, grad_router)


def solution(mesh):
    in_specs = (
        P(("expert", "hidden"), None, None),
        P(),
        P(("expert", "hidden"), None, None),
        P(("expert", "hidden"), None, None),
        P("expert", None, "hidden"),
        P("expert", None, "hidden"),
        P("expert", "hidden", None),
    )
    out_specs = (P(("expert", "hidden"), None, None), P(("expert", "hidden"), None))
    return jax.shard_map(shards, mesh=mesh, in_specs=in_specs, out_specs=out_specs, check_vma=False)
```

time: 832 us -> 119 us (0.14)
  waiting for transfers between devices: 700 us -> 55.1 us
  matrix products: 46.8 us -> 4.16 us
  blocking collectives: 28.6 us -> 0 us
  local copies, waits for them, and re-layouts: 28.7 us -> 3.49 us
  Pallas kernels: 0 us -> 23.8 us
  starting transfers between devices: 8.44 us -> 21.8 us
  between operations: 13.8 us -> 0.71 us
    unnamed x4 -> x0, waiting for transfers between devices: 628 us -> none
    all_to_all x1 -> x3, waiting for transfers between devices: 11.8 us -> 55.1 us  [exchange(): return lax.all_to_all(split, both, split_axis=0, concat_axis=0, tiled=True)]
    dot_general x8 -> x2, matrix products: 43 us -> 4.16 us  [the longest x1 2.41 us: shards(): jnp.einsum('bmn,dn->bmd', grad_logits, router, preferred_element_type=f32)]
    reduce_scatter x1 -> x0, waiting for transfers between devices: 35.4 us -> none  [shards(): lax.psum_scatter(partial_in.astype(jnp.bfloat16), 'hidden', scatter_dimen...]
    all_to_all x1 -> x0, blocking collectives: 28.6 us -> none  [shards(): lax.all_to_all(outbound, 'expert', split_axis=3, concat_axis=0, tiled=True)]
    all_gather x1 -> x0, waiting for transfers between devices: 24.9 us -> none  [shards(): paired = lax.all_gather(arrived, 'hidden', axis=1, tiled=True)]
    pallas_call x0 -> x4, Pallas kernels: none -> 23.8 us  [call(): kept(*[hold(x) if i is in_hbm else x for i, x in zip(ins, xs)])]
    convert_element_type x3 -> x0, local copies, waits for them, and re-layouts: 14.9 us -> none  [the longest x1 10.2 us: shards(): saved_pre.astype(jnp.float32)]
  transfers between devices with their start and end apart: 4 -> 3, of which waited for: 4 -> 3; matrix products, arithmetic and copies ran while one was open for 3% -> 10% of each run, Pallas kernels for 0% -> 2%
where the time goes in v2:
time: 119 us; the launch traced here: 118 us
  waiting for transfers between devices  55.1 us (46%)
  Pallas kernels  23.8 us (20%)
  starting transfers between devices  21.8 us (18%)
  other arithmetic  8.95 us (8%)
  matrix products  4.16 us (3%)
  local copies, waits for them, and re-layouts  3.49 us (3%)
    all_to_all x3, waiting for transfers between devices, exchange(): return lax.all_to_all(split, both, split_axis=0, concat_axis=0, tiled=True)  55.1 us
    pallas_call x4, Pallas kernels, call(): kept(*[hold(x) if i is in_hbm else x for i, x in zip(ins, xs)])  23.8 us
    all_to_all x3, starting transfers between devices, exchange(): return lax.all_to_all(split, both, split_axis=0, concat_axis=0, tiled=True)  21.8 us
    convert_element_type x1, other arithmetic, shards(): slope = gelu_slope(preact.astype(f32)).astype(bf16)  8.2 us
    unnamed x10, local copies, waits for them, and re-layouts  3.49 us
    dot_general x1, matrix products, shards(): jnp.einsum('bmn,dn->bmd', grad_logits, router, preferred_element_type=f32)  2.41 us
  transfers between devices with their start and end apart: 3, of which 3 were waited for; matrix products, arithmetic and copies ran while one was open for 10% of the time, Pallas kernels for 2%

profile of v2, /device:TPU:1, one launch (start us, length us, event | category | flops | bytes accessed | tf_op | source)
XLA Modules:
  0.0 118.0 jit_solution(35563766648068044)
XLA Ops:
  0.6 4.2 %slots.1 = (f32[2,256,256]{2,1,0:T(8,128)}, bf16[1024,1024]{1,0:T(8,128)(2,1)}) custom-call(bf16[2,256,1024]{2,1,0:T(8,128)(2,1)} %tokens_hbm.3, bf16[1024,256]{1,0:T(8,128)(2,1)} %router_hbm.1, bf16[2,256,1024]{2,1,0:T(8,128)(2,1)} %out_grad_ref.1), custom_call_target="tpu_custom_call" | custom-call | flops 536870912 | bytes 6291456 | tf_op jit(solution)/shard_map/slots/pallas_call | solution.py:224
  4.8 11.5 %all-to-all-start = ((bf16[128,8,1024]{2,1,0:T(8,128)(2,1)}), bf16[128,8,1024]{2,1,0:T(8,128)(2,1)S(1)}, u32[]{:S(2)}, u32[]{:S(2)}) async-start(bf16[128,8,1024]{2,1,0:T(8,128)(2,1)} %bitcast.14), calls=%async_computation | async-start | bytes 4194304 | tf_op jit(solution)/shard_map/all_to_all | solution.py:211
  16.3 8.2 %fusion.6.slope_hbm = bf16[2,512,2048]{2,1,0:T(8,128)(2,1)} fusion(bf16[2,512,2048]{2,1,0:T(8,128)(2,1)} %param.11), kind=kLoop, calls=%fused_computation.13 | loop fusion | flops 39845888 | bytes 8388608 | tf_op jit(solution)/shard_map/convert_element_type | solution.py:254
  24.5 21.5 %all-to-all-done = bf16[128,8,1024]{2,1,0:T(8,128)(2,1)S(1)} async-done(((bf16[128,8,1024]{2,1,0:T(8,128)(2,1)}), bf16[128,8,1024]{2,1,0:T(8,128)(2,1)S(1)}, u32[]{:S(2)}, u32[]{:S(2)}) %all-to-all-start) | async-done | bytes 2097184 | tf_op jit(solution)/shard_map/all_to_all | solution.py:211
  46.0 0.0 copy-start
  46.0 13.4 %experts.1 = bf16[1024,1024]{1,0:T(8,128)(2,1)} custom-call(bf16[1024,1024]{1,0:T(8,128)(2,1)S(1)} %bitcast.12, bf16[2,512,2048]{2,1,0:T(8,128)(2,1)} %fusion.6.slope_hbm, bf16[2,1024,2048]{2,1,0:T(8,128)(2,1)} %w_in_hbm.1, bf16[2,2048,1024]{2,1,0:T(8,128)(2,1)} %w_out_hbm.1), custom_call_target="tpu_custom_call" | custom-call | flops 8589934592 | bytes 25165824 | tf_op jit(solution)/shard_map/experts/pallas_call | solution.py:224
  59.4 5.1 %all-to-all-start.1 = ((bf16[128,8,1024]{2,1,0:T(8,128)(2,1)}), bf16[128,8,1024]{2,1,0:T(8,128)(2,1)S(1)}, u32[]{:S(2)}, u32[]{:S(2)}) async-start(bf16[128,8,1024]{2,1,0:T(8,128)(2,1)} %bitcast.13), calls=%async_computation.1 | async-start | bytes 4194304 | tf_op jit(solution)/shard_map/all_to_all | solution.py:211
  64.5 0.0 copy-done
  64.5 0.0 copy-start.1
  64.5 1.2 %copy-done.1 = bf16[2,256,1024]{2,1,0:T(8,128)(2,1)S(1)} copy-done((bf16[2,256,1024]{2,1,0:T(8,128)(2,1)S(1)}, bf16[2,256,1024]{2,1,0:T(8,128)(2,1)}, u32[]{:S(2)}) %copy-start.1) | copy-done | bytes 1048600
  65.8 0.0 copy-start.2
  65.8 1.2 %copy-done.2 = bf16[2,256,1024]{2,1,0:T(8,128)(2,1)S(1)} copy-done((bf16[2,256,1024]{2,1,0:T(8,128)(2,1)S(1)}, bf16[2,256,1024]{2,1,0:T(8,128)(2,1)}, u32[]{:S(2)}) %copy-start.2) | copy-done | bytes 1048600
  67.0 0.0 copy-start.3
  67.0 1.0 copy-done.3
  68.0 2.1 %combine.1 = (bf16[1024,512]{1,0:T(8,128)(2,1)}, f32[2,256,256]{2,1,0:T(8,128)}, bf16[2,256,256]{2,1,0:T(8,128)(2,1)}, f32[2,256,256]{2,1,0:T(8,128)}) custom-call(f32[2,256,256]{2,1,0:T(8,128)S(1)} %copy-done.3, bf16[2,256,1024]{2,1,0:T(8,128)(2,1)S(1)} %copy-done, bf16[2,256,1024]{2,1,0:T(8,128)(2,1)S(1)} %copy-done.1, bf16[2,256,1024]{2,1,0:T(8,128)(2,1)S(1)} %copy-done.2), custom_call_target="tpu_custom_call" | custom-call | flops 268435456 | bytes 8388608 | tf_op jit(solution)/shard_map/combine/pallas_call | solution.py:224
  70.2 0.0 copy-start.4
  70.2 24.0 %all-to-all-done.1 = bf16[128,8,1024]{2,1,0:T(8,128)(2,1)S(1)} async-done(((bf16[128,8,1024]{2,1,0:T(8,128)(2,1)}), bf16[128,8,1024]{2,1,0:T(8,128)(2,1)S(1)}, u32[]{:S(2)}, u32[]{:S(2)}) %all-to-all-start.1) | async-done | bytes 2097184 | tf_op jit(solution)/shard_map/all_to_all | solution.py:211
  94.2 4.1 %logit_grads.1 = (bf16[2,256,1024]{2,1,0:T(8,128)(2,1)}, bf16[2,256,256]{2,1,0:T(8,128)(2,1)}, bf16[1024,256]{1,0:T(8,128)(2,1)}) custom-call(bf16[1024,1024]{1,0:T(8,128)(2,1)S(1)} %bitcast.11, bf16[2,256,1024]{2,1,0:T(8,128)(2,1)} %tokens_hbm.3, bf16[1024,512]{1,0:T(8,128)(2,1)} %get-tuple-element.18.turned_hbm, ...), custom_call_target="tpu_custom_call" | custom-call | flops 805306368 | bytes 6291456 | tf_op jit(solution)/shard_map/logit_grads/pallas_call | solution.py:224
  98.4 5.1 %all-to-all-start.2 = ((bf16[128,8,256]{2,1,0:T(8,128)(2,1)}), bf16[128,8,256]{2,1,0:T(8,128)(2,1)S(1)}, u32[]{:S(2)}, u32[]{:S(2)}) async-start(bf16[128,8,256]{2,1,0:T(8,128)(2,1)} %bitcast.15), calls=%async_computation.2 | async-start | bytes 1048576 | tf_op jit(solution)/shard_map/all_to_all | solution.py:211
  103.5 1.8 %fusion.9 = f32[2,256,1024]{2,1,0:T(8,128)S(1)} fusion(bf16[2,256,256]{2,1,0:T(8,128)(2,1)} %get-tuple-element.17, bf16[2,256,1024]{2,1,0:T(8,128)(2,1)} %get-tuple-element.21), kind=kOutput, calls=%fused_computation.18 | convolution fusion | flops 268435456 | bytes 3407872 | tf_op jit(solution)/shard_map/bmn,bnd->bmd/dot_general | solution.py:311
  105.3 0.0 copy-done.4
  105.3 2.4 %add_convert_fusion = bf16[2,256,1024]{2,1,0:T(8,128)(2,1)} fusion(f32[2,256,1024]{2,1,0:T(8,128)S(1)} %fusion.9, bf16[2,256,256]{2,1,0:T(8,128)(2,1)} %get-tuple-element.22, bf16[1024,256]{1,0:T(8,128)(2,1)S(1)} %copy-done.4), kind=kOutput, calls=%fused_computation.15 | convolution fusion | flops 269484032 | bytes 3932160 | tf_op jit(solution)/shard_map/bmn,dn->bmd/dot_general | solution.py:312
  107.7 9.6 %all-to-all-done.2 = bf16[128,8,256]{2,1,0:T(8,128)(2,1)S(1)} async-done(((bf16[128,8,256]{2,1,0:T(8,128)(2,1)}), bf16[128,8,256]{2,1,0:T(8,128)(2,1)S(1)}, u32[]{:S(2)}, u32[]{:S(2)}) %all-to-all-start.2) | async-done | bytes 524320 | tf_op jit(solution)/shard_map/all_to_all | solution.py:211
  117.3 0.8 multiply_reduce_fusion
Async XLA Ops:
  4.8 41.2 %all-to-all-start = ((bf16[128,8,1024]{2,1,0:T(8,128)(2,1)}), bf16[128,8,1024]{2,1,0:T(8,128)(2,1)S(1)}, u32[]{:S(2)}, u32[]{:S(2)}) async-start(bf16[128,8,1024]{2,1,0:T(8,128)(2,1)} %bitcast.14), calls=%async_computation | async-start | bytes 4194304 | tf_op jit(solution)/shard_map/all_to_all | solution.py:211
  46.0 18.5 %copy-start = (bf16[2,256,1024]{2,1,0:T(8,128)(2,1)S(1)}, bf16[2,256,1024]{2,1,0:T(8,128)(2,1)}, u32[]{:S(2)}) copy-start(bf16[2,256,1024]{2,1,0:T(8,128)(2,1)} %tokens_hbm.3) | copy-start | bytes 3145732
  59.4 34.8 %all-to-all-start.1 = ((bf16[128,8,1024]{2,1,0:T(8,128)(2,1)}), bf16[128,8,1024]{2,1,0:T(8,128)(2,1)S(1)}, u32[]{:S(2)}, u32[]{:S(2)}) async-start(bf16[128,8,1024]{2,1,0:T(8,128)(2,1)} %bitcast.13), calls=%async_computation.1 | async-start | bytes 4194304 | tf_op jit(solution)/shard_map/all_to_all | solution.py:211
  64.5 1.2 %copy-start.1 = (bf16[2,256,1024]{2,1,0:T(8,128)(2,1)S(1)}, bf16[2,256,1024]{2,1,0:T(8,128)(2,1)}, u32[]{:S(2)}) copy-start(bf16[2,256,1024]{2,1,0:T(8,128)(2,1)} %out_grad_ref.1) | copy-start | bytes 3145732
  65.8 1.2 %copy-start.2 = (bf16[2,256,1024]{2,1,0:T(8,128)(2,1)S(1)}, bf16[2,256,1024]{2,1,0:T(8,128)(2,1)}, u32[]{:S(2)}) copy-start(bf16[2,256,1024]{2,1,0:T(8,128)(2,1)} %slot_outputs_ref.1) | copy-start | bytes 3145732
  67.0 1.0 copy-start.3
  70.2 35.1 %copy-start.4 = (bf16[1024,256]{1,0:T(8,128)(2,1)S(1)}, bf16[1024,256]{1,0:T(8,128)(2,1)}, u32[]{:S(2)}) copy-start(bf16[1024,256]{1,0:T(8,128)(2,1)} %router_hbm.1) | copy-start | bytes 1572868
  98.4 18.9 %all-to-all-start.2 = ((bf16[128,8,256]{2,1,0:T(8,128)(2,1)}), bf16[128,8,256]{2,1,0:T(8,128)(2,1)S(1)}, u32[]{:S(2)}, u32[]{:S(2)}) async-start(bf16[128,8,256]{2,1,0:T(8,128)(2,1)} %bitcast.15), calls=%async_computation.2 | async-start | bytes 1048576 | tf_op jit(solution)/shard_map/all_to_all | solution.py:211

commit v3 on v2

--- a/solution.py
+++ b/solution.py
@@ -12,7 +12,6 @@
 bf16 = jnp.bfloat16
 f32 = jnp.float32
 block = 256
-vmem_bytes = 40 * 1024 * 1024
 in_hbm = pl.BlockSpec(memory_space=pl.ANY)
 in_vmem = pl.BlockSpec(memory_space=pltpu.VMEM)
 
@@ -41,8 +40,8 @@
 
 
 def slots_kernel(
-    tokens_hbm, router_hbm, out_grad_hbm, logits_hbm, send_hbm, tokens, router, out_grad, logits_kept, slot_grad, send,
-    sems, send_sems, *, images, rows, n_hid, exp_dev, per
+    tokens_hbm, router_hbm, out_grad_hbm, logits_hbm, send_ref, tokens, router, out_grad, logits_kept, slot_grad,
+    sems, send_sem, *, images, rows, n_hid, exp_dev, per
 ):
     loads = [pltpu.make_async_copy(router_hbm, router, sems.at[2 * images])]
     loads += [pltpu.make_async_copy(tokens_hbm.at[i], tokens.at[i], sems.at[i]) for i in range(images)]
@@ -68,36 +67,16 @@
         exp, img, s = at // (images * per), (at // per) % images, at % per
         return img * take + dest * own + exp * per + s
 
+    copy = pltpu.make_async_copy(logits_kept, logits_hbm, send_sem)
+    copy.start()
     pick = one_hot(block, images * take, source)
-    copies = []
-    for k in range(send.shape[0] // block):
+    for k in range(send_ref.shape[0] // block):
         parts = [slot_grad[m, k * take : (k + 1) * take, :] for m in range(images)]
-        at = pl.ds(k * block, block)
-        send[at, :] = mm(pick, jnp.concatenate(parts, axis=0)).astype(bf16)
-        copies.append(pltpu.make_async_copy(send.at[at], send_hbm.at[at], send_sems.at[k]))
-        copies[-1].start()
-    copies.append(pltpu.make_async_copy(logits_kept, logits_hbm, send_sems.at[len(copies)]))
-    copies[-1].start()
-    for copy in copies:
-        copy.wait()
-
-
-def experts_kernel(
-    recv_ref, slope_hbm, w_in_hbm, w_out_hbm, send_hbm, slope, w_in, w_out, grads, grad_pre, back, send, sems, send_sems,
-    *, exp_dev, rows
-):
-    hid = slope.shape[2]
-    first = [pl.ds(0, hid // 4), pl.ds(hid // 4, hid // 4), pl.ds(hid // 2, hid // 2)]
-    units = [first] + [[pl.ds(0, hid)]] * (exp_dev - 1)
-    loads = []
-    for e in range(exp_dev):
-        for at in units[e]:
-            loads.append((w_out_hbm.at[e, at], w_out.at[e, at]))
-            loads.append((slope_hbm.at[e, :, at], slope.at[e, :, at]))
-        loads.append((w_in_hbm.at[e], w_in.at[e]))
-    loads = [pltpu.make_async_copy(a, b, sems.at[n]) for n, (a, b) in enumerate(loads)]
-    for load in loads:
-        load.start()
+        send_ref[k * block : (k + 1) * block, :] = mm(pick, jnp.concatenate(parts, axis=0)).astype(bf16)
+    copy.wait()
+
+
+def experts_kernel(recv_ref, preact_ref, w_in_ref, w_out_ref, send_hbm, grads, grad_pre, back, send, send_sems, *, exp_dev, rows):
     own = rows // exp_dev
     take = block // exp_dev
     blocks = recv_ref.shape[0] // block
@@ -106,17 +85,12 @@
         picked = mm(pick, recv_ref[k * block : (k + 1) * block, :]).astype(bf16)
         for e in range(exp_dev):
             grads[e, k * take : (k + 1) * take, :] = picked[e * take : (e + 1) * take, :]
-    n = 0
     for e in range(exp_dev):
-        for at in units[e]:
-            loads[n].wait()
-            loads[n + 1].wait()
-            grad_act = mm(grads[e], w_out[e, at, :], 1, 1)
-            grad_pre[:, at] = (grad_act * slope[e, :, at].astype(f32)).astype(bf16)
-            n += 2
-        loads[n].wait()
-        back[e] = mm(grad_pre[...], w_in[e], 1, 1).astype(bf16)
-        n += 1
+        for k in range(w_out_ref.shape[1] // block):
+            at = slice(k * block, (k + 1) * block)
+            grad_act = mm(grads[e], w_out_ref[e, at, :], 1, 1)
+            grad_pre[:, at] = (grad_act * gelu_slope(preact_ref[e, :, at].astype(f32))).astype(bf16)
+        back[e] = mm(grad_pre[...], w_in_ref[e], 1, 1).astype(bf16)
     pick = one_hot(block, block, lambda r: (r % rows // own) * take + r // rows * own + r % own)
     copies = []
     for k in range(blocks):
@@ -210,14 +184,14 @@
         split = x.reshape(devs, -1, x.shape[1])
         return lax.all_to_all(split, both, split_axis=0, concat_axis=0, tiled=True)
 
-    def call(kernel, ins, outs, outs_in, scratch, flops, moved, name):
+    def call(kernel, ins, outs, outs_in, scratch, flops, moved, name, mebibytes=40, near=()):
         kept = pl.pallas_call(
             kernel,
             in_specs=ins,
-            out_specs=[outs_in] * len(outs),
-            out_shape=[pltpu.HBM(*o) for o in outs],
+            out_specs=[in_vmem if n in near else outs_in for n in range(len(outs))],
+            out_shape=[(pltpu.VMEM if n in near else pltpu.HBM)(*o) for n, o in enumerate(outs)],
             scratch_shapes=scratch,
-            compiler_params=pltpu.CompilerParams(vmem_limit_bytes=vmem_bytes),
+            compiler_params=pltpu.CompilerParams(vmem_limit_bytes=mebibytes << 20),
             cost_estimate=pl.CostEstimate(flops=flops, transcendentals=0, bytes_accessed=moved),
             name=name,
         )
@@ -240,39 +214,35 @@
             pltpu.VMEM(out_grad.shape, bf16),
             pltpu.VMEM(logit_shape, f32),
             pltpu.VMEM(slot_shape, bf16),
-            pltpu.VMEM((all_rows, feat), bf16),
             dma((2 * images + 1,)),
-            dma((1 + all_rows // block,)),
+            dma,
         ],
-        2 * per_image,
+        40 * per_image,
         6 << 20,
         "slots",
+        12,
+        (1,),
     )(tokens, router, out_grad)
 
     arrived = exchange(send)
-    preact, _ = lax.optimization_barrier((preact, send))
-    slope = gelu_slope(preact.astype(f32)).astype(bf16)
-
+    preact, w_in, w_out = [pltpu.with_memory_space_constraint(x, pltpu.VMEM) for x in (preact, w_in, w_out)]
     partial_in = call(
         functools.partial(experts_kernel, exp_dev=exp_dev, rows=rows),
-        [in_vmem] + [in_hbm] * 3,
+        [in_vmem] * 4,
         [((all_rows, feat), bf16)],
         in_hbm,
         [
-            pltpu.VMEM(preact.shape, bf16),
-            pltpu.VMEM(w_in.shape, bf16),
-            pltpu.VMEM(w_out.shape, bf16),
             pltpu.VMEM((exp_dev, exp_rows, feat), bf16),
             pltpu.VMEM((exp_rows, hid), bf16),
             pltpu.VMEM((exp_dev, exp_rows, feat), bf16),
             pltpu.VMEM((all_rows, feat), bf16),
-            dma((3 * exp_dev + 4,)),
             dma((all_rows // block,)),
         ],
         4 * exp_dev * exp_rows * feat * hid,
-        24 << 20,
+        4 << 20,
         "experts",
-    )(arrived.reshape(all_rows, feat), slope, w_in, w_out)[0]
+        24,
+    )(arrived.reshape(all_rows, feat), preact, w_in, w_out)[0]
 
     returned = exchange(partial_in)
     logits, _ = lax.optimization_barrier((logits, partial_in))

time: 119 us -> 117 us (0.983)
  blocking collectives: 0 us -> 41 us
  waiting for transfers between devices: 55.1 us -> 34.6 us
  starting transfers between devices: 21.8 us -> 10.3 us
  other arithmetic: 8.95 us -> 0.75 us
  Pallas kernels: 23.8 us -> 22.5 us
    all_to_all x0 -> x1, blocking collectives: none -> 41 us  [exchange(): return lax.all_to_all(split, both, split_axis=0, concat_axis=0, tiled=True)]
    all_to_all x3 -> x2, waiting for transfers between devices: 55.1 us -> 34.6 us  [exchange(): return lax.all_to_all(split, both, split_axis=0, concat_axis=0, tiled=True)]
    all_to_all x3 -> x2, starting transfers between devices: 21.8 us -> 10.3 us  [exchange(): return lax.all_to_all(split, both, split_axis=0, concat_axis=0, tiled=True)]
    convert_element_type x1 -> x0, other arithmetic: 8.2 us -> none  [shards(): slope = gelu_slope(preact.astype(f32)).astype(bf16)]
    pallas_call x4, Pallas kernels: 23.8 us -> 22.5 us  [call(): kept(*[hold(x) if i is in_hbm else x for i, x in zip(ins, xs)])]
    unnamed x10 -> x20, local copies, waits for them, and re-layouts: 3.49 us -> 3.52 us
  transfers between devices with their start and end apart: 3 -> 2, of which waited for: 3 -> 2; matrix products, arithmetic and copies ran while one was open for 10% -> 3% of each run, Pallas kernels for 2% -> 2%
where the time goes in v3:
time: 117 us
  blocking collectives  41 us (35%)
  waiting for transfers between devices  34.6 us (30%)
  Pallas kernels  22.5 us (19%)
  starting transfers between devices  10.3 us (9%)
  local copies, waits for them, and re-layouts  3.52 us (3%)
  matrix products  3.12 us (3%)
    all_to_all x1, blocking collectives, exchange(): return lax.all_to_all(split, both, split_axis=0, concat_axis=0, tiled=True)  41 us
    all_to_all x2, waiting for transfers between devices, exchange(): return lax.all_to_all(split, both, split_axis=0, concat_axis=0, tiled=True)  34.6 us
    pallas_call x4, Pallas kernels, call(): kept(*[hold(x) if i is in_hbm else x for i, x in zip(ins, xs)])  22.5 us
    all_to_all x2, starting transfers between devices, exchange(): return lax.all_to_all(split, both, split_axis=0, concat_axis=0, tiled=True)  10.3 us
    unnamed x20, local copies, waits for them, and re-layouts  3.52 us
  transfers between devices with their start and end apart: 2, of which 2 were waited for; matrix products, arithmetic and copies ran while one was open for 3% of the time, Pallas kernels for 2%

profile of v3, /device:TPU:1, one launch (start us, length us, event | category | flops | bytes accessed | tf_op | source)
XLA Modules:
  0.0 116.6 jit_solution(7879397406158497259)
XLA Ops:
  0.6 0.0 copy-start.4
  0.6 0.0 copy-start.5
  0.6 3.2 %slots.1 = (f32[2,256,256]{2,1,0:T(8,128)}, bf16[1024,1024]{1,0:T(8,128)(2,1)S(1)}) custom-call(bf16[2,256,1024]{2,1,0:T(8,128)(2,1)} %tokens_hbm.3, bf16[1024,256]{1,0:T(8,128)(2,1)} %router_hbm.1, bf16[2,256,1024]{2,1,0:T(8,128)(2,1)} %out_grad_ref.1), custom_call_target="tpu_custom_call" | custom-call | flops 10737418240 | bytes 6291456 | tf_op jit(solution)/shard_map/slots/pallas_call | solution.py:198
  3.9 0.0 copy-start.6
  3.9 41.0 %all_to_all.15 = bf16[128,8,1024]{2,1,0:T(8,128)(2,1)S(1)} all-to-all(bf16[128,8,1024]{2,1,0:T(8,128)(2,1)S(1)} %bitcast.12), channel_id=1, replica_groups=mesh['expert'=64,'hidden'=2] {'expert','hidden'}, dimensions={0} | all-to-all | bytes 4194304 | tf_op jit(solution)/shard_map/all_to_all | solution.py:185
  44.9 0.0 copy-done.4
  44.9 0.0 copy-done.5
  44.9 0.0 copy-done.6
  44.9 13.0 %experts.1 = bf16[1024,1024]{1,0:T(8,128)(2,1)} custom-call(bf16[1024,1024]{1,0:T(8,128)(2,1)S(1)} %bitcast.13, bf16[2,512,2048]{2,1,0:T(8,128)(2,1)S(1)} %copy-done.6, bf16[2,1024,2048]{2,1,0:T(8,128)(2,1)S(1)} %copy-done.4, bf16[2,2048,1024]{2,1,0:T(8,128)(2,1)S(1)} %copy-done.5), custom_call_target="tpu_custom_call" | custom-call | flops 8589934592 | bytes 4194304 | tf_op jit(solution)/shard_map/experts/pallas_call | solution.py:198
  57.9 0.0 copy-start
  57.9 5.1 %all-to-all-start.1 = ((bf16[128,8,1024]{2,1,0:T(8,128)(2,1)}), bf16[128,8,1024]{2,1,0:T(8,128)(2,1)S(1)}, u32[]{:S(2)}, u32[]{:S(2)}) async-start(bf16[128,8,1024]{2,1,0:T(8,128)(2,1)} %bitcast.14), calls=%async_computation.1 | async-start | bytes 4194304 | tf_op jit(solution)/shard_map/all_to_all | solution.py:185
  63.1 0.0 copy-done
  63.1 0.0 copy-start.1
  63.1 1.2 %copy-done.1 = bf16[2,256,1024]{2,1,0:T(8,128)(2,1)S(1)} copy-done((bf16[2,256,1024]{2,1,0:T(8,128)(2,1)S(1)}, bf16[2,256,1024]{2,1,0:T(8,128)(2,1)}, u32[]{:S(2)}) %copy-start.1) | copy-done | bytes 1048600
  64.3 0.0 copy-start.2
  64.3 1.2 %copy-done.2 = bf16[2,256,1024]{2,1,0:T(8,128)(2,1)S(1)} copy-done((bf16[2,256,1024]{2,1,0:T(8,128)(2,1)S(1)}, bf16[2,256,1024]{2,1,0:T(8,128)(2,1)}, u32[]{:S(2)}) %copy-start.2) | copy-done | bytes 1048600
  65.5 0.0 copy-start.3
  65.5 1.0 copy-done.3
  66.6 2.1 %combine.1 = (bf16[1024,512]{1,0:T(8,128)(2,1)}, f32[2,256,256]{2,1,0:T(8,128)}, bf16[2,256,256]{2,1,0:T(8,128)(2,1)}, f32[2,256,256]{2,1,0:T(8,128)}) custom-call(f32[2,256,256]{2,1,0:T(8,128)S(1)} %copy-done.3, bf16[2,256,1024]{2,1,0:T(8,128)(2,1)S(1)} %copy-done, bf16[2,256,1024]{2,1,0:T(8,128)(2,1)S(1)} %copy-done.1, bf16[2,256,1024]{2,1,0:T(8,128)(2,1)S(1)} %copy-done.2), custom_call_target="tpu_custom_call" | custom-call | flops 268435456 | bytes 8388608 | tf_op jit(solution)/shard_map/combine/pallas_call | solution.py:198
  68.7 24.0 %all-to-all-done.1 = bf16[128,8,1024]{2,1,0:T(8,128)(2,1)S(1)} async-done(((bf16[128,8,1024]{2,1,0:T(8,128)(2,1)}), bf16[128,8,1024]{2,1,0:T(8,128)(2,1)S(1)}, u32[]{:S(2)}, u32[]{:S(2)}) %all-to-all-start.1) | async-done | bytes 2097184 | tf_op jit(solution)/shard_map/all_to_all | solution.py:185
  92.8 0.0 copy-start.8
  92.8 4.2 %logit_grads.1 = (bf16[2,256,1024]{2,1,0:T(8,128)(2,1)}, bf16[2,256,256]{2,1,0:T(8,128)(2,1)}, bf16[1024,256]{1,0:T(8,128)(2,1)}) custom-call(bf16[1024,1024]{1,0:T(8,128)(2,1)S(1)} %bitcast.11, bf16[2,256,1024]{2,1,0:T(8,128)(2,1)} %tokens_hbm.3, bf16[1024,512]{1,0:T(8,128)(2,1)} %get-tuple-element.16.turned_hbm, ...), custom_call_target="tpu_custom_call" | custom-call | flops 805306368 | bytes 6291456 | tf_op jit(solution)/shard_map/logit_grads/pallas_call | solution.py:198
  97.0 0.0 copy-start.7
  97.0 0.0 copy-start.9
  97.0 5.1 %all-to-all-start.2 = ((bf16[128,8,256]{2,1,0:T(8,128)(2,1)}), bf16[128,8,256]{2,1,0:T(8,128)(2,1)S(1)}, u32[]{:S(2)}, u32[]{:S(2)}) async-start(bf16[128,8,256]{2,1,0:T(8,128)(2,1)} %bitcast.15), calls=%async_computation.2 | async-start | bytes 1048576 | tf_op jit(solution)/shard_map/all_to_all | solution.py:185
  102.1 0.0 copy-done.8
  102.1 1.7 %fusion.1 = f32[2,256,1024]{2,1,0:T(8,128)S(1)} fusion(bf16[2,256,256]{2,1,0:T(8,128)(2,1)S(1)} %copy-done.8, bf16[2,256,1024]{2,1,0:T(8,128)(2,1)} %get-tuple-element.19), kind=kOutput, calls=%fused_computation.3 | convolution fusion | flops 268435456 | bytes 3407872 | tf_op jit(solution)/shard_map/bmn,bnd->bmd/dot_general | solution.py:281
  103.8 0.0 copy-done.7
  103.8 0.0 copy-done.9
  103.8 1.5 %add_convert_fusion = bf16[2,256,1024]{2,1,0:T(8,128)(2,1)} fusion(f32[2,256,1024]{2,1,0:T(8,128)S(1)} %fusion.1, bf16[2,256,256]{2,1,0:T(8,128)(2,1)S(1)} %copy-done.9, bf16[1024,256]{1,0:T(8,128)(2,1)S(1)} %copy-done.7), kind=kOutput, calls=%fused_computation | convolution fusion | flops 269484032 | bytes 3932160 | tf_op jit(solution)/shard_map/bmn,dn->bmd/dot_general | solution.py:282
  105.3 10.6 %all-to-all-done.2 = bf16[128,8,256]{2,1,0:T(8,128)(2,1)S(1)} async-done(((bf16[128,8,256]{2,1,0:T(8,128)(2,1)}), bf16[128,8,256]{2,1,0:T(8,128)(2,1)S(1)}, u32[]{:S(2)}, u32[]{:S(2)}) %all-to-all-start.2) | async-done | bytes 524320 | tf_op jit(solution)/shard_map/all_to_all | solution.py:185
  115.9 0.8 multiply_reduce_fusion
Async XLA Ops:
  0.6 44.3 %copy-start.4 = (bf16[2,1024,2048]{2,1,0:T(8,128)(2,1)S(1)}, bf16[2,1024,2048]{2,1,0:T(8,128)(2,1)}, u32[]{:S(2)}) copy-start(bf16[2,1024,2048]{2,1,0:T(8,128)(2,1)} %w_in_ref.1) | copy-start | bytes 25165828
  0.6 44.2 %copy-start.5 = (bf16[2,2048,1024]{2,1,0:T(8,128)(2,1)S(1)}, bf16[2,2048,1024]{2,1,0:T(8,128)(2,1)}, u32[]{:S(2)}) copy-start(bf16[2,2048,1024]{2,1,0:T(8,128)(2,1)} %w_out_ref.1) | copy-start | bytes 25165828
  3.9 41.0 %copy-start.6 = (bf16[2,512,2048]{2,1,0:T(8,128)(2,1)S(1)}, bf16[2,512,2048]{2,1,0:T(8,128)(2,1)}, u32[]{:S(2)}) copy-start(bf16[2,512,2048]{2,1,0:T(8,128)(2,1)} %preact_ref.1) | copy-start | bytes 12582916
  57.9 5.2 %copy-start = (bf16[2,256,1024]{2,1,0:T(8,128)(2,1)S(1)}, bf16[2,256,1024]{2,1,0:T(8,128)(2,1)}, u32[]{:S(2)}) copy-start(bf16[2,256,1024]{2,1,0:T(8,128)(2,1)} %tokens_hbm.3) | copy-start | bytes 3145732
  57.9 34.8 %all-to-all-start.1 = ((bf16[128,8,1024]{2,1,0:T(8,128)(2,1)}), bf16[128,8,1024]{2,1,0:T(8,128)(2,1)S(1)}, u32[]{:S(2)}, u32[]{:S(2)}) async-start(bf16[128,8,1024]{2,1,0:T(8,128)(2,1)} %bitcast.14), calls=%async_computation.1 | async-start | bytes 4194304 | tf_op jit(solution)/shard_map/all_to_all | solution.py:185
  63.1 1.2 %copy-start.1 = (bf16[2,256,1024]{2,1,0:T(8,128)(2,1)S(1)}, bf16[2,256,1024]{2,1,0:T(8,128)(2,1)}, u32[]{:S(2)}) copy-start(bf16[2,256,1024]{2,1,0:T(8,128)(2,1)} %out_grad_ref.1) | copy-start | bytes 3145732
  64.3 1.2 %copy-start.2 = (bf16[2,256,1024]{2,1,0:T(8,128)(2,1)S(1)}, bf16[2,256,1024]{2,1,0:T(8,128)(2,1)}, u32[]{:S(2)}) copy-start(bf16[2,256,1024]{2,1,0:T(8,128)(2,1)} %slot_outputs_ref.1) | copy-start | bytes 3145732
  65.5 1.0 copy-start.3
  92.8 9.4 %copy-start.8 = (bf16[2,256,256]{2,1,0:T(8,128)(2,1)S(1)}, bf16[2,256,256]{2,1,0:T(8,128)(2,1)}, u32[]{:S(2)}) copy-start(bf16[2,256,256]{2,1,0:T(8,128)(2,1)} %get-tuple-element.15) | copy-start | bytes 786436
  97.0 6.8 %copy-start.7 = (bf16[1024,256]{1,0:T(8,128)(2,1)S(1)}, bf16[1024,256]{1,0:T(8,128)(2,1)}, u32[]{:S(2)}) copy-start(bf16[1024,256]{1,0:T(8,128)(2,1)} %router_hbm.1) | copy-start | bytes 1572868
  97.0 6.8 %copy-start.9 = (bf16[2,256,256]{2,1,0:T(8,128)(2,1)S(1)}, bf16[2,256,256]{2,1,0:T(8,128)(2,1)}, u32[]{:S(2)}) copy-start(bf16[2,256,256]{2,1,0:T(8,128)(2,1)} %get-tuple-element.20) | copy-start | bytes 786436
  97.0 18.9 %all-to-all-start.2 = ((bf16[128,8,256]{2,1,0:T(8,128)(2,1)}), bf16[128,8,256]{2,1,0:T(8,128)(2,1)S(1)}, u32[]{:S(2)}, u32[]{:S(2)}) async-start(bf16[128,8,256]{2,1,0:T(8,128)(2,1)} %bitcast.15), calls=%async_computation.2 | async-start | bytes 1048576 | tf_op jit(solution)/shard_map/all_to_all | solution.py:185

commit v4 on v3

--- a/solution.py
+++ b/solution.py
@@ -85,12 +85,17 @@
         picked = mm(pick, recv_ref[k * block : (k + 1) * block, :]).astype(bf16)
         for e in range(exp_dev):
             grads[e, k * take : (k + 1) * take, :] = picked[e * take : (e + 1) * take, :]
-    for e in range(exp_dev):
-        for k in range(w_out_ref.shape[1] // block):
+    units, feats = w_out_ref.shape[1] // block, w_out_ref.shape[2] // block
+    for e in range(exp_dev + 1):
+        for k in range(units):
             at = slice(k * block, (k + 1) * block)
-            grad_act = mm(grads[e], w_out_ref[e, at, :], 1, 1)
-            grad_pre[:, at] = (grad_act * gelu_slope(preact_ref[e, :, at].astype(f32))).astype(bf16)
-        back[e] = mm(grad_pre[...], w_in_ref[e], 1, 1).astype(bf16)
+            if e < exp_dev:
+                grad_act = mm(grads[e], w_out_ref[e, at, :], 1, 1)
+                grad_pre[e, :, at] = (grad_act * gelu_slope(preact_ref[e, :, at].astype(f32))).astype(bf16)
+                if 0 < e and k < feats:
+                    back[e - 1, :, at] = mm(grad_pre[e - 1], w_in_ref[e - 1, at, :], 1, 1).astype(bf16)
+        if e == exp_dev:
+            back[e - 1] = mm(grad_pre[e - 1], w_in_ref[e - 1], 1, 1).astype(bf16)
     pick = one_hot(block, block, lambda r: (r % rows // own) * take + r // rows * own + r % own)
     copies = []
     for k in range(blocks):
@@ -233,7 +238,7 @@
         in_hbm,
         [
             pltpu.VMEM((exp_dev, exp_rows, feat), bf16),
-            pltpu.VMEM((exp_rows, hid), bf16),
+            pltpu.VMEM((exp_dev, exp_rows, hid), bf16),
             pltpu.VMEM((exp_dev, exp_rows, feat), bf16),
             pltpu.VMEM((all_rows, feat), bf16),
             dma((all_rows // block,)),
@@ -241,7 +246,7 @@
         4 * exp_dev * exp_rows * feat * hid,
         4 << 20,
         "experts",
-        24,
+        28,
     )(arrived.reshape(all_rows, feat), preact, w_in, w_out)[0]
 
     returned = exchange(partial_in)

time: 117 us -> 116 us (level)
  no operation moved by 1% of the time
where the time goes in v4:
time: 116 us
  blocking collectives  41 us (35%)
  waiting for transfers between devices  34.6 us (30%)
  Pallas kernels  22 us (19%)
  starting transfers between devices  10.3 us (9%)
  local copies, waits for them, and re-layouts  3.52 us (3%)
  matrix products  3.12 us (3%)
    all_to_all x1, blocking collectives, exchange(): return lax.all_to_all(split, both, split_axis=0, concat_axis=0, tiled=True)  41 us
    all_to_all x2, waiting for transfers between devices, exchange(): return lax.all_to_all(split, both, split_axis=0, concat_axis=0, tiled=True)  34.6 us
    pallas_call x4, Pallas kernels, call(): kept(*[hold(x) if i is in_hbm else x for i, x in zip(ins, xs)])  22 us
    all_to_all x2, starting transfers between devices, exchange(): return lax.all_to_all(split, both, split_axis=0, concat_axis=0, tiled=True)  10.3 us
    unnamed x20, local copies, waits for them, and re-layouts  3.52 us
  transfers between devices with their start and end apart: 2, of which 2 were waited for; matrix products, arithmetic and copies ran while one was open for 3% of the time, Pallas kernels for 2%

profile of v4, /device:TPU:1, one launch (start us, length us, event | category | flops | bytes accessed | tf_op | source)
XLA Modules:
  0.0 116.1 jit_solution(11497044513204837410)
XLA Ops:
  0.6 0.0 copy-start.4
  0.6 0.0 copy-start.5
  0.6 3.2 %slots.1 = (f32[2,256,256]{2,1,0:T(8,128)}, bf16[1024,1024]{1,0:T(8,128)(2,1)S(1)}) custom-call(bf16[2,256,1024]{2,1,0:T(8,128)(2,1)} %tokens_hbm.3, bf16[1024,256]{1,0:T(8,128)(2,1)} %router_hbm.1, bf16[2,256,1024]{2,1,0:T(8,128)(2,1)} %out_grad_ref.1), custom_call_target="tpu_custom_call" | custom-call | flops 10737418240 | bytes 6291456 | tf_op jit(solution)/shard_map/slots/pallas_call | solution.py:203
  3.9 0.0 copy-start.6
  3.9 41.0 %all_to_all.15 = bf16[128,8,1024]{2,1,0:T(8,128)(2,1)S(1)} all-to-all(bf16[128,8,1024]{2,1,0:T(8,128)(2,1)S(1)} %bitcast.12), channel_id=1, replica_groups=mesh['expert'=64,'hidden'=2] {'expert','hidden'}, dimensions={0} | all-to-all | bytes 4194304 | tf_op jit(solution)/shard_map/all_to_all | solution.py:190
  44.9 0.0 copy-done.4
  44.9 0.0 copy-done.5
  44.9 0.0 copy-done.6
  44.9 12.5 %experts.1 = bf16[1024,1024]{1,0:T(8,128)(2,1)} custom-call(bf16[1024,1024]{1,0:T(8,128)(2,1)S(1)} %bitcast.13, bf16[2,512,2048]{2,1,0:T(8,128)(2,1)S(1)} %copy-done.6, bf16[2,1024,2048]{2,1,0:T(8,128)(2,1)S(1)} %copy-done.4, bf16[2,2048,1024]{2,1,0:T(8,128)(2,1)S(1)} %copy-done.5), custom_call_target="tpu_custom_call" | custom-call | flops 8589934592 | bytes 4194304 | tf_op jit(solution)/shard_map/experts/pallas_call | solution.py:203
  57.4 0.0 copy-start
  57.4 5.1 %all-to-all-start.1 = ((bf16[128,8,1024]{2,1,0:T(8,128)(2,1)}), bf16[128,8,1024]{2,1,0:T(8,128)(2,1)S(1)}, u32[]{:S(2)}, u32[]{:S(2)}) async-start(bf16[128,8,1024]{2,1,0:T(8,128)(2,1)} %bitcast.14), calls=%async_computation.1 | async-start | bytes 4194304 | tf_op jit(solution)/shard_map/all_to_all | solution.py:190
  62.5 0.0 copy-done
  62.5 0.0 copy-start.1
  62.5 1.2 %copy-done.1 = bf16[2,256,1024]{2,1,0:T(8,128)(2,1)S(1)} copy-done((bf16[2,256,1024]{2,1,0:T(8,128)(2,1)S(1)}, bf16[2,256,1024]{2,1,0:T(8,128)(2,1)}, u32[]{:S(2)}) %copy-start.1) | copy-done | bytes 1048600
  63.8 0.0 copy-start.2
  63.8 1.2 %copy-done.2 = bf16[2,256,1024]{2,1,0:T(8,128)(2,1)S(1)} copy-done((bf16[2,256,1024]{2,1,0:T(8,128)(2,1)S(1)}, bf16[2,256,1024]{2,1,0:T(8,128)(2,1)}, u32[]{:S(2)}) %copy-start.2) | copy-done | bytes 1048600
  65.0 0.0 copy-start.3
  65.0 1.0 copy-done.3
  66.0 2.1 %combine.1 = (bf16[1024,512]{1,0:T(8,128)(2,1)}, f32[2,256,256]{2,1,0:T(8,128)}, bf16[2,256,256]{2,1,0:T(8,128)(2,1)}, f32[2,256,256]{2,1,0:T(8,128)}) custom-call(f32[2,256,256]{2,1,0:T(8,128)S(1)} %copy-done.3, bf16[2,256,1024]{2,1,0:T(8,128)(2,1)S(1)} %copy-done, bf16[2,256,1024]{2,1,0:T(8,128)(2,1)S(1)} %copy-done.1, bf16[2,256,1024]{2,1,0:T(8,128)(2,1)S(1)} %copy-done.2), custom_call_target="tpu_custom_call" | custom-call | flops 268435456 | bytes 8388608 | tf_op jit(solution)/shard_map/combine/pallas_call | solution.py:203
  68.2 24.0 %all-to-all-done.1 = bf16[128,8,1024]{2,1,0:T(8,128)(2,1)S(1)} async-done(((bf16[128,8,1024]{2,1,0:T(8,128)(2,1)}), bf16[128,8,1024]{2,1,0:T(8,128)(2,1)S(1)}, u32[]{:S(2)}, u32[]{:S(2)}) %all-to-all-start.1) | async-done | bytes 2097184 | tf_op jit(solution)/shard_map/all_to_all | solution.py:190
  92.2 0.0 copy-start.8
  92.2 4.2 %logit_grads.1 = (bf16[2,256,1024]{2,1,0:T(8,128)(2,1)}, bf16[2,256,256]{2,1,0:T(8,128)(2,1)}, bf16[1024,256]{1,0:T(8,128)(2,1)}) custom-call(bf16[1024,1024]{1,0:T(8,128)(2,1)S(1)} %bitcast.11, bf16[2,256,1024]{2,1,0:T(8,128)(2,1)} %tokens_hbm.3, bf16[1024,512]{1,0:T(8,128)(2,1)} %get-tuple-element.16.turned_hbm, ...), custom_call_target="tpu_custom_call" | custom-call | flops 805306368 | bytes 6291456 | tf_op jit(solution)/shard_map/logit_grads/pallas_call | solution.py:203
  96.4 0.0 copy-start.7
  96.4 0.0 copy-start.9
  96.4 5.1 %all-to-all-start.2 = ((bf16[128,8,256]{2,1,0:T(8,128)(2,1)}), bf16[128,8,256]{2,1,0:T(8,128)(2,1)S(1)}, u32[]{:S(2)}, u32[]{:S(2)}) async-start(bf16[128,8,256]{2,1,0:T(8,128)(2,1)} %bitcast.15), calls=%async_computation.2 | async-start | bytes 1048576 | tf_op jit(solution)/shard_map/all_to_all | solution.py:190
  101.6 0.0 copy-done.8
  101.6 1.7 %fusion.1 = f32[2,256,1024]{2,1,0:T(8,128)S(1)} fusion(bf16[2,256,256]{2,1,0:T(8,128)(2,1)S(1)} %copy-done.8, bf16[2,256,1024]{2,1,0:T(8,128)(2,1)} %get-tuple-element.19), kind=kOutput, calls=%fused_computation.3 | convolution fusion | flops 268435456 | bytes 3407872 | tf_op jit(solution)/shard_map/bmn,bnd->bmd/dot_general | solution.py:286
  103.2 0.0 copy-done.7
  103.3 0.0 copy-done.9
  103.3 1.5 %add_convert_fusion = bf16[2,256,1024]{2,1,0:T(8,128)(2,1)} fusion(f32[2,256,1024]{2,1,0:T(8,128)S(1)} %fusion.1, bf16[2,256,256]{2,1,0:T(8,128)(2,1)S(1)} %copy-done.9, bf16[1024,256]{1,0:T(8,128)(2,1)S(1)} %copy-done.7), kind=kOutput, calls=%fused_computation | convolution fusion | flops 269484032 | bytes 3932160 | tf_op jit(solution)/shard_map/bmn,dn->bmd/dot_general | solution.py:287
  104.7 10.6 %all-to-all-done.2 = bf16[128,8,256]{2,1,0:T(8,128)(2,1)S(1)} async-done(((bf16[128,8,256]{2,1,0:T(8,128)(2,1)}), bf16[128,8,256]{2,1,0:T(8,128)(2,1)S(1)}, u32[]{:S(2)}, u32[]{:S(2)}) %all-to-all-start.2) | async-done | bytes 524320 | tf_op jit(solution)/shard_map/all_to_all | solution.py:190
  115.3 0.8 multiply_reduce_fusion
Async XLA Ops:
  0.6 44.3 %copy-start.4 = (bf16[2,1024,2048]{2,1,0:T(8,128)(2,1)S(1)}, bf16[2,1024,2048]{2,1,0:T(8,128)(2,1)}, u32[]{:S(2)}) copy-start(bf16[2,1024,2048]{2,1,0:T(8,128)(2,1)} %w_in_ref.1) | copy-start | bytes 25165828
  0.6 44.2 %copy-start.5 = (bf16[2,2048,1024]{2,1,0:T(8,128)(2,1)S(1)}, bf16[2,2048,1024]{2,1,0:T(8,128)(2,1)}, u32[]{:S(2)}) copy-start(bf16[2,2048,1024]{2,1,0:T(8,128)(2,1)} %w_out_ref.1) | copy-start | bytes 25165828
  3.9 41.0 %copy-start.6 = (bf16[2,512,2048]{2,1,0:T(8,128)(2,1)S(1)}, bf16[2,512,2048]{2,1,0:T(8,128)(2,1)}, u32[]{:S(2)}) copy-start(bf16[2,512,2048]{2,1,0:T(8,128)(2,1)} %preact_ref.1) | copy-start | bytes 12582916
  57.4 5.2 %copy-start = (bf16[2,256,1024]{2,1,0:T(8,128)(2,1)S(1)}, bf16[2,256,1024]{2,1,0:T(8,128)(2,1)}, u32[]{:S(2)}) copy-start(bf16[2,256,1024]{2,1,0:T(8,128)(2,1)} %tokens_hbm.3) | copy-start | bytes 3145732
  57.4 34.8 %all-to-all-start.1 = ((bf16[128,8,1024]{2,1,0:T(8,128)(2,1)}), bf16[128,8,1024]{2,1,0:T(8,128)(2,1)S(1)}, u32[]{:S(2)}, u32[]{:S(2)}) async-start(bf16[128,8,1024]{2,1,0:T(8,128)(2,1)} %bitcast.14), calls=%async_computation.1 | async-start | bytes 4194304 | tf_op jit(solution)/shard_map/all_to_all | solution.py:190
  62.5 1.2 %copy-start.1 = (bf16[2,256,1024]{2,1,0:T(8,128)(2,1)S(1)}, bf16[2,256,1024]{2,1,0:T(8,128)(2,1)}, u32[]{:S(2)}) copy-start(bf16[2,256,1024]{2,1,0:T(8,128)(2,1)} %out_grad_ref.1) | copy-start | bytes 3145732
  63.8 1.2 %copy-start.2 = (bf16[2,256,1024]{2,1,0:T(8,128)(2,1)S(1)}, bf16[2,256,1024]{2,1,0:T(8,128)(2,1)}, u32[]{:S(2)}) copy-start(bf16[2,256,1024]{2,1,0:T(8,128)(2,1)} %slot_outputs_ref.1) | copy-start | bytes 3145732
  65.0 1.0 copy-start.3
  92.2 9.4 %copy-start.8 = (bf16[2,256,256]{2,1,0:T(8,128)(2,1)S(1)}, bf16[2,256,256]{2,1,0:T(8,128)(2,1)}, u32[]{:S(2)}) copy-start(bf16[2,256,256]{2,1,0:T(8,128)(2,1)} %get-tuple-element.15) | copy-start | bytes 786436
  96.4 6.8 %copy-start.7 = (bf16[1024,256]{1,0:T(8,128)(2,1)S(1)}, bf16[1024,256]{1,0:T(8,128)(2,1)}, u32[]{:S(2)}) copy-start(bf16[1024,256]{1,0:T(8,128)(2,1)} %router_hbm.1) | copy-start | bytes 1572868
  96.4 6.8 %copy-start.9 = (bf16[2,256,256]{2,1,0:T(8,128)(2,1)S(1)}, bf16[2,256,256]{2,1,0:T(8,128)(2,1)}, u32[]{:S(2)}) copy-start(bf16[2,256,256]{2,1,0:T(8,128)(2,1)} %get-tuple-element.20) | copy-start | bytes 786436
  96.4 18.9 %all-to-all-start.2 = ((bf16[128,8,256]{2,1,0:T(8,128)(2,1)}), bf16[128,8,256]{2,1,0:T(8,128)(2,1)S(1)}, u32[]{:S(2)}, u32[]{:S(2)}) async-start(bf16[128,8,256]{2,1,0:T(8,128)(2,1)} %bitcast.15), calls=%async_computation.2 | async-start | bytes 1048576 | tf_op jit(solution)/shard_map/all_to_all | solution.py:190
